TPU v7x, 128 devices: a whole 4x4x4 slice. The times are simulated.
128 devices in a mesh: wide: 16 (over z, x), narrow: 8 (over y, core).
Axes of the slice: x: 4, y: 4, z: 4, core: 2. Of those that a mesh axis runs over, the one named last changes fastest.
Arguments:
- inputs: bfloat16 [4, 256, 16384], P(None, 'wide', 'narrow'), may hold values from -600 to 600
- norm_gain: bfloat16 [16384], P('narrow'), may hold values from 0.099609375 to 1.8984375
- w_query: bfloat16 [16384, 8192], P('narrow', 'wide'), may hold values from -0.0234375 to 0.0234375
- w_keyval: bfloat16 [16384, 1024], P('narrow', 'wide'), may hold values from -0.0234375 to 0.0234375
- w_out: bfloat16 [8192, 16384], P('wide', 'narrow'), may hold values from -0.0625 to 0.0625
- key_cache: bfloat16 [256, 4096, 512], P(('wide', 'narrow')), may hold values from -1700 to 1700
- value_cache: bfloat16 [256, 4096, 512], P(('wide', 'narrow')), may hold values from -48 to 48
- lengths: int32 [256], P(('wide', 'narrow')), may hold values from 1024 to 4092, as said below
- positions: int32 [256], P(('wide', 'narrow')), may hold values from 1024 to 8187, as said below
Outputs:
- attended: bfloat16 [4, 256, 16384], P(None, 'wide', 'narrow')
- new_keys: bfloat16 [4, 256, 512], P(None, ('wide', 'narrow'))
- new_values: bfloat16 [4, 256, 512], P(None, ('wide', 'narrow'))
Inputs may be any that keep to these rules, and one draw needn't show every extreme that they name: A row's cache holds its first lengths slots. `positions`: a row's later new tokens follow its first one position by position.
All inputs are finite; a program needn't handle non-finite values.
Results may differ from a plain program's by a relative error of at most 0.007.
The roundings to bfloat16 on the way count: a program that leaves them out, or rounds other values in their place, can miss the bound.
Values may be sent and summed in bfloat16 or wider, within the bound.
A program may use at most 128 MiB of HBM per device.

v0:
```python
import jax
import jax.numpy as jnp
from jax import lax
from jax.sharding import PartitionSpec as P

D = 16384
HQ = 64
KVH = 4
HD = 128
STEPS = 4


def rotate(values, rotary_pos):
    half_dim = values.shape[-1] // 2
    inverse_freq = jnp.exp(
        -jnp.log(jnp.float32(500000.0))
        * jnp.arange(half_dim, dtype=jnp.float32)
        * 2.0
        / (2 * half_dim)
    )
    angles = rotary_pos.astype(jnp.float32)[..., None] * inverse_freq
    cosine = jnp.cos(angles)[..., None, :]
    sine = jnp.sin(angles)[..., None, :]
    first_half = values[..., :half_dim]
    second_half = values[..., half_dim:]
    return jnp.concatenate(
        [first_half * cosine - second_half * sine, second_half * cosine + first_half * sine],
        axis=-1,
    )


def local(inputs, norm_gain, w_query, w_keyval, w_out, key_cache, value_cache, lengths, positions):
    wide_count = lax.axis_size("wide")
    narrow_count = lax.axis_size("narrow")
    rows_dev = key_cache.shape[0]
    cache_len = key_cache.shape[1]
    q_local = w_query.shape[1]
    kv_local = w_keyval.shape[1]
    col_count = q_local + kv_local
    group_size = HQ // KVH
    factor = 1.0 / jnp.sqrt(jnp.float32(HD))
    step_outputs = []
    key_list = []
    value_list = []
    for step_index in range(STEPS):
        prepare_step_block = inputs[step_index : step_index + 1]
        project_count_steps = prepare_step_block.shape[0]
        row_values = prepare_step_block.astype(jnp.float32)
        partial_square = jnp.sum(row_values * row_values, axis=-1)
        total_square = lax.psum(partial_square, "narrow")
        inv_rms = lax.rsqrt(total_square / D + 1e-05)
        normed = (row_values * inv_rms[..., None] * norm_gain.astype(jnp.float32)).astype(
            jnp.bfloat16
        )
        shard_piece = lax.all_gather(normed, "wide", axis=1, tiled=True)
        first_part = jnp.einsum(
            "trd,dc->trc", shard_piece, w_query, preferred_element_type=jnp.float32
        )
        second_part = jnp.einsum(
            "trd,dc->trc", shard_piece, w_keyval, preferred_element_type=jnp.float32
        )
        project_partials = jnp.concatenate([first_part, second_part], axis=2)
        split_terms = project_partials.reshape(
            project_count_steps, wide_count, narrow_count, rows_dev, col_count
        )
        summed = lax.psum_scatter(split_terms, "narrow", scatter_dimension=2, tiled=True).astype(
            jnp.bfloat16
        )
        summed = summed.reshape(project_count_steps, wide_count, rows_dev, col_count)
        received = lax.all_to_all(summed, "wide", split_axis=1, concat_axis=3, tiled=True)
        arranged = received.reshape(project_count_steps, rows_dev, wide_count, col_count)
        query = arranged[..., :q_local].reshape(project_count_steps, rows_dev, HQ * HD)
        keyval = arranged[..., q_local:].reshape(project_count_steps, rows_dev, 2 * KVH * HD)
        prepare_count_steps = prepare_step_block.shape[0]
        rotary_pos = (
            positions[None, :]
            + step_index
            + jnp.arange(prepare_count_steps, dtype=jnp.int32)[:, None]
        )
        prepare_rot_query = rotate(
            query.astype(jnp.float32).reshape(prepare_count_steps, rows_dev, HQ, HD), rotary_pos
        )
        prepare_rot_query = prepare_rot_query.astype(jnp.bfloat16).reshape(
            prepare_count_steps, rows_dev, HQ * HD
        )
        rot_keys = rotate(
            keyval[..., : KVH * HD]
            .astype(jnp.float32)
            .reshape(prepare_count_steps, rows_dev, KVH, HD),
            rotary_pos,
        )
        rot_keys = rot_keys.astype(jnp.bfloat16).reshape(prepare_count_steps, rows_dev, KVH * HD)
        rot_query, rot_keys, new_vals = (prepare_rot_query, rot_keys, keyval[..., KVH * HD :])
        key_list.append(rot_keys)
        value_list.append(new_vals)
        fresh_keys = jnp.concatenate(key_list, axis=0)
        attend_count_steps = rot_query.shape[0]
        fresh_count = fresh_keys.shape[0]
        grouped = rot_query.reshape(attend_count_steps, rows_dev, KVH, group_size, HD)
        cached = key_cache.reshape(rows_dev, cache_len, KVH, HD)
        cache_scores = (
            jnp.einsum("trgqd,rsgd->rgtqs", grouped, cached, preferred_element_type=jnp.float32)
            * factor
        )
        visible = jnp.arange(cache_len, dtype=jnp.int32)[None, :] < lengths[:, None]
        cache_scores = jnp.where(visible[:, None, None, None, :], cache_scores, -jnp.inf)
        fresh_view = fresh_keys.reshape(fresh_count, rows_dev, KVH, HD)
        fresh_scores = (
            jnp.einsum("trgqd,jrgd->rgtqj", grouped, fresh_view, preferred_element_type=jnp.float32)
            * factor
        )
        causal_mask = (
            jnp.arange(fresh_count, dtype=jnp.int32)[None, :]
            <= (step_index + jnp.arange(attend_count_steps, dtype=jnp.int32))[:, None]
        )
        fresh_scores = jnp.where(causal_mask[None, None, :, None, :], fresh_scores, -jnp.inf)
        highest = jnp.maximum(jnp.max(cache_scores, -1), jnp.max(fresh_scores, -1))[..., None]
        cache_exp = jnp.exp(cache_scores - highest)
        fresh_exp = jnp.exp(fresh_scores - highest)
        normaliser = jnp.sum(cache_exp, -1, keepdims=True) + jnp.sum(fresh_exp, -1, keepdims=True)
        cache_weights = (cache_exp / normaliser).astype(jnp.bfloat16)
        fresh_weights = (fresh_exp / normaliser).astype(jnp.bfloat16)
        cached_values = value_cache.reshape(rows_dev, cache_len, KVH, HD)
        fresh_vals = jnp.concatenate(value_list, axis=0).reshape(fresh_count, rows_dev, KVH, HD)
        output = jnp.einsum(
            "rgtqs,rsgd->trgqd", cache_weights, cached_values, preferred_element_type=jnp.float32
        )
        output = output + jnp.einsum(
            "rgtqj,jrgd->trgqd", fresh_weights, fresh_vals, preferred_element_type=jnp.float32
        )
        attended_heads = output.astype(jnp.bfloat16).reshape(attend_count_steps, rows_dev, HQ * HD)
        count_steps = attended_heads.shape[0]
        by_heads = lax.all_to_all(
            attended_heads.reshape(count_steps, 1, rows_dev, HQ * HD),
            "wide",
            split_axis=3,
            concat_axis=1,
            tiled=True,
        )
        by_heads = by_heads.reshape(count_steps, wide_count, 1, rows_dev, by_heads.shape[-1])
        partials = jnp.einsum(
            "twprh,hc->twprc",
            lax.all_gather(by_heads, "narrow", axis=2, tiled=True),
            w_out,
            preferred_element_type=jnp.float32,
        )
        partials = partials.reshape(
            count_steps, wide_count * narrow_count * rows_dev, partials.shape[-1]
        )
        step_outputs.append(
            lax.psum_scatter(partials, "wide", scatter_dimension=1, tiled=True).astype(jnp.bfloat16)
        )
    return (
        jnp.concatenate(step_outputs, axis=0),
        jnp.concatenate(key_list, axis=0),
        jnp.concatenate(value_list, axis=0),
    )


def solution(mesh):
    return jax.shard_map(
        local,
        mesh=mesh,
        in_specs=(
            P(None, "wide", "narrow"),
            P("narrow"),
            P("narrow", "wide"),
            P("narrow", "wide"),
            P("wide", "narrow"),
            P(("wide", "narrow"), None, None),
            P(("wide", "narrow"), None, None),
            P(("wide", "narrow")),
            P(("wide", "narrow")),
        ),
        out_specs=(
            P(None, "wide", "narrow"),
            P(None, ("wide", "narrow"), None),
            P(None, ("wide", "narrow"), None),
        ),
        check_vma=False,
    )
```

profile of v0, /device:TPU:0, one launch (start us, length us, event | category | flops | bytes accessed | tf_op | source)
XLA Modules:
  0.0 833.2 jit_solution(438713747634489099)
XLA Ops:
  9.2 15.0 %all-reduce = (f32[1,16]{1,0:T(1,128)S(1)}, f32[1,16]{1,0:T(1,128)S(1)}, f32[1,16]{1,0:T(1,128)S(1)}, f32[1,16]{1,0:T(1,128)S(1)}) all-reduce(f32[1,16]{1,0:T(1,128)S(1)} %bitcast.378, f32[1,16]{1,0:T(1,128)S(1)} %bitcast.379, f32[1,16]{1,0:T(1,128)S(1)} %bitcast.377, ...), channel_id=1, replica_groups=mesh['wide'=16,'narrow'=8] {'narrow'}, use_global_device_ids=true, to_apply=%region_23.24 | all-reduce | flops 64 | bytes 512 | tf_op jit(solution)/shard_map/psum | solution.py:50
  28.1 40.4 %all-gather.7.cloned.1.call-done = bf16[1,256,2048]{2,1,0:T(8,128)(2,1)} async-done(((bf16[1,16,2048]{2,1,0:T(8,128)(2,1)}), bf16[1,256,2048]{2,1,0:T(8,128)(2,1)}) %all-gather.7.cloned.1.call-update) | async-done | bytes 1048592 | tf_op jit(solution)/shard_map/all_gather | solution.py:55
  74.2 38.9 %all-gather.5.cloned.1.call-done = bf16[1,256,2048]{2,1,0:T(8,128)(2,1)} async-done(((bf16[1,16,2048]{2,1,0:T(8,128)(2,1)}), bf16[1,256,2048]{2,1,0:T(8,128)(2,1)}) %all-gather.5.cloned.1.call-update) | async-done | bytes 1048592 | tf_op jit(solution)/shard_map/all_gather | solution.py:55
  119.0 38.2 %all-gather.11.cloned.1.call-done = bf16[1,256,2048]{2,1,0:T(8,128)(2,1)} async-done(((bf16[1,16,2048]{2,1,0:T(8,128)(2,1)}), bf16[1,256,2048]{2,1,0:T(8,128)(2,1)}) %all-gather.11.cloned.1.call-update) | async-done | bytes 1048592 | tf_op jit(solution)/shard_map/all_gather | solution.py:55
  163.0 38.1 %all-gather.9.cloned.1.call-done = bf16[1,256,2048]{2,1,0:T(8,128)(2,1)} async-done(((bf16[1,16,2048]{2,1,0:T(8,128)(2,1)}), bf16[1,256,2048]{2,1,0:T(8,128)(2,1)}) %all-gather.9.cloned.1.call-update) | async-done | bytes 1048592 | tf_op jit(solution)/shard_map/all_gather | solution.py:55
  206.7 27.4 %reduce-scatter.13.cloned.1.call-done = f32[1,16,1,2,576]{4,1,3,0,2:T(8,128)} async-done(((f32[1,16,8,2,576]{4,1,3,0,2:T(8,128)}), f32[1,16,1,2,576]{4,1,3,0,2:T(8,128)}) %reduce-scatter.13.cloned.1.call-update) | async-done | bytes 73744 | tf_op jit(solution)/shard_map/reduce_scatter | solution.py:66
  242.6 24.2 %reduce-scatter.9.cloned.1.call-done = f32[1,16,1,2,576]{4,1,3,0,2:T(8,128)} async-done(((f32[1,16,8,2,576]{4,1,3,0,2:T(8,128)}), f32[1,16,1,2,576]{4,1,3,0,2:T(8,128)}) %reduce-scatter.9.cloned.1.call-update) | async-done | bytes 73744 | tf_op jit(solution)/shard_map/reduce_scatter | solution.py:66
  302.3 46.5 %reduce.42 = bf16[8192,2]{1,0:T(8,128)(2,1)} reduce(bf16[8192,1,1,2]{3,2,1,0:T(2,128)(2,1)} %bitcast.332, bf16[]{:T(256)} %broadcast.355), dimensions={1,2}, to_apply=%bitcast.274.reduce_sub_computation | reduce | bytes 65538
  368.2 8.4 %reshape.1214 = bf16[8192,1,1,2]{3,2,1,0:T(2,128)(2,1)} reshape(bf16[16,2,512]{2,1,0:T(2,128)(2,1)S(1)} %all-to-all-done.3) | data formatting | bytes 65536
  376.6 8.1 copy.244
  384.7 12.8 %all_gather.27 = bf16[1,16,8,2,512]{4,1,3,0,2:T(8,128)(2,1)S(1)} all-gather(bf16[1,16,1,2,512]{4,1,3,0,2:T(8,128)(2,1)S(1)} %bitcast.368), channel_id=1, replica_groups=mesh['wide'=16,'narrow'=8] {'narrow'}, dimensions={2}, use_global_device_ids=true | all-gather | bytes 294912 | tf_op jit(solution)/shard_map/all_gather | solution.py:143
  435.4 46.6 %reduce.40 = bf16[8192,2]{1,0:T(8,128)(2,1)} reduce(bf16[8192,1,1,2]{3,2,1,0:T(2,128)(2,1)} %bitcast.335, bf16[]{:T(256)} %broadcast.355), dimensions={1,2}, to_apply=%bitcast.270.reduce_sub_computation | reduce | bytes 65538
  486.2 10.7 %all_to_all.120 = bf16[16,2,512]{2,1,0:T(2,128)(2,1)S(1)} all-to-all(bf16[16,2,512]{2,1,0:T(2,128)(2,1)S(1)} %reshape.1209), channel_id=1, replica_groups=mesh['wide'=16,'narrow'=8] {'wide'}, dimensions={0} | all-to-all | bytes 65536 | tf_op jit(solution)/shard_map/all_to_all | solution.py:133
  496.9 8.4 %reshape.1210 = bf16[8192,1,1,2]{3,2,1,0:T(2,128)(2,1)} reshape(bf16[16,2,512]{2,1,0:T(2,128)(2,1)S(1)} %all_to_all.120) | data formatting | bytes 65536
  513.4 13.0 %all_gather.31 = bf16[1,16,8,2,512]{4,1,3,0,2:T(8,128)(2,1)S(1)} all-gather(bf16[1,16,1,2,512]{4,1,3,0,2:T(8,128)(2,1)S(1)} %bitcast.369), channel_id=1, replica_groups=mesh['wide'=16,'narrow'=8] {'narrow'}, dimensions={2}, use_global_device_ids=true | all-gather | bytes 294912 | tf_op jit(solution)/shard_map/all_gather | solution.py:143
  547.5 46.6 %reduce.41 = bf16[8192,2]{1,0:T(8,128)(2,1)} reduce(bf16[8192,1,1,2]{3,2,1,0:T(2,128)(2,1)} %bitcast.337, bf16[]{:T(256)} %broadcast.355), dimensions={1,2}, to_apply=%bitcast.272.reduce_sub_computation | reduce | bytes 65538
  598.3 10.8 %all_to_all.121 = bf16[16,2,512]{2,1,0:T(2,128)(2,1)S(1)} all-to-all(bf16[16,2,512]{2,1,0:T(2,128)(2,1)S(1)} %reshape.1211), channel_id=1, replica_groups=mesh['wide'=16,'narrow'=8] {'wide'}, dimensions={0} | all-to-all | bytes 65536 | tf_op jit(solution)/shard_map/all_to_all | solution.py:133
  609.1 8.4 %reshape.1212 = bf16[8192,1,1,2]{3,2,1,0:T(2,128)(2,1)} reshape(bf16[16,2,512]{2,1,0:T(2,128)(2,1)S(1)} %all_to_all.121) | data formatting | bytes 65536
  625.6 13.1 %all_gather.29 = bf16[1,16,8,2,512]{4,1,3,0,2:T(8,128)(2,1)S(1)} all-gather(bf16[1,16,1,2,512]{4,1,3,0,2:T(8,128)(2,1)S(1)} %bitcast.370), channel_id=1, replica_groups=mesh['wide'=16,'narrow'=8] {'narrow'}, dimensions={2}, use_global_device_ids=true | all-gather | bytes 294912 | tf_op jit(solution)/shard_map/all_gather | solution.py:143
  659.6 46.5 %reduce.43 = bf16[8192,2]{1,0:T(8,128)(2,1)} reduce(bf16[8192,1,1,2]{3,2,1,0:T(2,128)(2,1)} %bitcast.333, bf16[]{:T(256)} %broadcast.355), dimensions={1,2}, to_apply=%bitcast.276.reduce_sub_computation | reduce | bytes 65538
  710.2 10.8 %all_to_all.122 = bf16[16,2,512]{2,1,0:T(2,128)(2,1)S(1)} all-to-all(bf16[16,2,512]{2,1,0:T(2,128)(2,1)S(1)} %reshape.1215), channel_id=1, replica_groups=mesh['wide'=16,'narrow'=8] {'wide'}, dimensions={0} | all-to-all | bytes 65536 | tf_op jit(solution)/shard_map/all_to_all | solution.py:133
  721.0 8.4 %reshape.1216 = bf16[8192,1,1,2]{3,2,1,0:T(2,128)(2,1)} reshape(bf16[16,2,512]{2,1,0:T(2,128)(2,1)S(1)} %all_to_all.122) | data formatting | bytes 65536
  737.5 12.8 %all_gather.25 = bf16[1,16,8,2,512]{4,1,3,0,2:T(8,128)(2,1)S(1)} all-gather(bf16[1,16,1,2,512]{4,1,3,0,2:T(8,128)(2,1)S(1)} %bitcast.371), channel_id=1, replica_groups=mesh['wide'=16,'narrow'=8] {'narrow'}, dimensions={2}, use_global_device_ids=true | all-gather | bytes 294912 | tf_op jit(solution)/shard_map/all_gather | solution.py:143
  756.3 68.0 %reduce-scatter.11.cloned.1.call-done = f32[1,16,2048]{2,1,0:T(8,128)} async-done(((f32[1,256,2048]{2,1,0:T(8,128)}), f32[1,16,2048]{2,1,0:T(8,128)}) %reduce-scatter.11.cloned.1.call-update) | async-done | bytes 131088 | tf_op jit(solution)/shard_map/reduce_scatter | solution.py:151
  (211 shorter events, 215.8 us)
Async XLA Ops:
  7.2 390.8 %copy-start = (bf16[512,2048]{1,0:T(8,128)(2,1)S(1)}, bf16[512,2048]{1,0:T(8,128)(2,1)}, u32[]{:S(2)}) copy-start(bf16[512,2048]{1,0:T(8,128)(2,1)} %param.13) | copy-start | bytes 6291460
  7.2 63.1 %copy-start.4 = (bf16[2048,64]{0,1:T(8,128)(2,1)S(1)}, bf16[2048,64]{0,1:T(8,128)(2,1)}, u32[]{:S(2)}) copy-start(bf16[2048,64]{0,1:T(8,128)(2,1)} %param.12) | copy-start | bytes 786436
  7.2 61.3 %all-gather.7.cloned.1.call-start = ((), (), s32[]{:S(2)}) async-start(), calls=%async_computation.19 | async-start | bytes 1114112 | tf_op jit(solution)/shard_map/all_gather | solution.py:55
  26.0 87.1 %all-gather.5.cloned.1.call-start = ((), (), s32[]{:S(2)}) async-start(), calls=%async_computation.16 | async-start | bytes 1114112 | tf_op jit(solution)/shard_map/all_gather | solution.py:55
  26.7 130.5 %all-gather.11.cloned.1.call-start = ((), (), s32[]{:S(2)}) async-start(), calls=%async_computation.25 | async-start | bytes 1114112 | tf_op jit(solution)/shard_map/all_gather | solution.py:55
  27.4 173.6 %all-gather.9.cloned.1.call-start = ((), (), s32[]{:S(2)}) async-start(), calls=%async_computation.22 | async-start | bytes 1114112 | tf_op jit(solution)/shard_map/all_gather | solution.py:55
  28.0 206.1 %reduce-scatter.13.cloned.1.call-start = ((), (), s32[]{:S(2)}) async-start(), calls=%async_computation.20 | async-start | bytes 737280 | tf_op jit(solution)/shard_map/reduce_scatter | solution.py:66
  74.1 192.6 %reduce-scatter.9.cloned.1.call-start = ((), (), s32[]{:S(2)}) async-start(), calls=%async_computation.17 | async-start | bytes 737280 | tf_op jit(solution)/shard_map/reduce_scatter | solution.py:66
  117.6 1.2 copy-start.2
  118.8 238.4 %reduce-scatter.21.cloned.1.call-start = ((), (), s32[]{:S(2)}) async-start(), calls=%async_computation.26 | async-start | bytes 737280 | tf_op jit(solution)/shard_map/reduce_scatter | solution.py:66
  161.7 1.2 copy-start.3
  162.8 237.2 %reduce-scatter.17.cloned.1.call-start = ((), (), s32[]{:S(2)}) async-start(), calls=%async_computation.23 | async-start | bytes 737280 | tf_op jit(solution)/shard_map/reduce_scatter | solution.py:66
  235.7 32.6 %all-to-all-start.2 = ((bf16[1,16,2,576]{3,2,0,1:T(2,128)(2,1)}), bf16[1,16,2,576]{3,2,0,1:T(2,128)(2,1)S(1)}, u32[]{:S(2)}, u32[]{:S(2)}) async-start(bf16[1,16,2,576]{3,2,0,1:T(2,128)(2,1)} %copy.238), calls=%async_computation.5 | async-start | bytes 81920 | tf_op jit(solution)/shard_map/all_to_all | solution.py:70
  268.3 14.7 %all-to-all-start = ((bf16[1,16,2,576]{3,2,0,1:T(2,128)(2,1)}), bf16[1,16,2,576]{3,2,0,1:T(2,128)(2,1)S(1)}, u32[]{:S(2)}, u32[]{:S(2)}) async-start(bf16[1,16,2,576]{3,2,0,1:T(2,128)(2,1)} %copy.226), calls=%async_computation.1 | async-start | bytes 81920 | tf_op jit(solution)/shard_map/all_to_all | solution.py:70
  353.6 11.0 %all-to-all-start.3 = ((bf16[16,2,512]{2,1,0:T(2,128)(2,1)}), bf16[16,2,512]{2,1,0:T(2,128)(2,1)S(1)}, u32[]{:S(2)}, u32[]{:S(2)}) async-start(bf16[16,2,512]{2,1,0:T(2,128)(2,1)} %reshape.1213), calls=%async_computation.6 | async-start | bytes 65536 | tf_op jit(solution)/shard_map/all_to_all | solution.py:133
  364.7 36.9 %all-to-all-start.6 = ((bf16[1,16,2,576]{3,2,0,1:T(2,128)(2,1)}), bf16[1,16,2,576]{3,2,0,1:T(2,128)(2,1)S(1)}, u32[]{:S(2)}, u32[]{:S(2)}) async-start(bf16[1,16,2,576]{3,2,0,1:T(2,128)(2,1)} %copy.264), calls=%async_computation.13 | async-start | bytes 81920 | tf_op jit(solution)/shard_map/all_to_all | solution.py:70
  368.2 385.3 %reduce-scatter.15.cloned.1.call-start = ((), (), s32[]{:S(2)}) async-start(), calls=%async_computation.21 | async-start | bytes 2228224 | tf_op jit(solution)/shard_map/reduce_scatter | solution.py:151
  401.6 14.8 %all-to-all-start.4 = ((bf16[1,16,2,576]{3,2,0,1:T(2,128)(2,1)}), bf16[1,16,2,576]{3,2,0,1:T(2,128)(2,1)S(1)}, u32[]{:S(2)}, u32[]{:S(2)}) async-start(bf16[1,16,2,576]{3,2,0,1:T(2,128)(2,1)} %copy.251), calls=%async_computation.9 | async-start | bytes 81920 | tf_op jit(solution)/shard_map/all_to_all | solution.py:70
  408.8 345.7 %reduce-scatter.23.cloned.1.call-start = ((), (), s32[]{:S(2)}) async-start(), calls=%async_computation.27 | async-start | bytes 2228224 | tf_op jit(solution)/shard_map/reduce_scatter | solution.py:151
  416.5 6.6 copy-start.1
  528.9 226.5 %reduce-scatter.19.cloned.1.call-start = ((), (), s32[]{:S(2)}) async-start(), calls=%async_computation.24 | async-start | bytes 2228224 | tf_op jit(solution)/shard_map/reduce_scatter | solution.py:151
  641.1 183.2 %reduce-scatter.11.cloned.1.call-start = ((), (), s32[]{:S(2)}) async-start(), calls=%async_computation.18 | async-start | bytes 2228224 | tf_op jit(solution)/shard_map/reduce_scatter | solution.py:151
Sparse Core Ops, SparseCore 0:
  26.1 42.3 all-gather.6
  71.2 41.8 all-gather.4
  115.3 41.8 all-gather.10
  159.2 41.8 all-gather.8
  203.3 30.8 reduce-scatter.12
  236.4 30.2 reduce-scatter.8
  269.1 30.2 reduce-scatter.20
  301.8 30.5 reduce-scatter.16
  400.2 75.4 reduce-scatter.14
  529.0 71.2 reduce-scatter.22
  641.2 71.4 reduce-scatter.18
  752.9 71.2 reduce-scatter.10
where the time goes:
time: 842 us; the launch traced here: 833 us
  waiting for transfers between devices  297 us (35%)
  other arithmetic  202 us (24%)
  local copies, waits for them, and re-layouts  127 us (15%)
  blocking collectives  99 us (12%)
  matrix products  63.4 us (8%)
  starting transfers between devices  29 us (3%)
  between operations  15.4 us (2%)
    unnamed x4, other arithmetic  186 us
    all_gather x4, waiting for transfers between devices, local(): shard_piece = lax.all_gather(normed, 'wide', axis=1, tiled=True)  156 us
    reduce_scatter x4, waiting for transfers between devices, local(): lax.psum_scatter(partials, 'wide', scatter_dimension=1, tiled=True)  68 us
    all_gather x4, blocking collectives, local(): lax.all_gather(by_heads, 'narrow', axis=2, tiled=True)  51.7 us
    reduce_scatter x4, waiting for transfers between devices, local(): lax.psum_scatter(split_terms, 'narrow', scatter_dimension=2, tiled=True)  51.6 us
    unnamed x25, local copies, waits for them, and re-layouts  51.4 us
    all_to_all x3, blocking collectives, local(): lax.all_to_all(attended_heads.reshape(count_steps, 1, rows_dev, HQ * HD),...  32.3 us
    all_to_all x4, local copies, waits for them, and re-layouts, local(): lax.all_to_all(attended_heads.reshape(count_steps, 1, rows_dev, HQ * HD),...  32.3 us
  transfers between devices with their start and end apart: 17, of which 10 were waited for; matrix products, arithmetic and copies ran while one was open for 46% of the time, Pallas kernels for 0%

commit v1 on v0

v1 whole, which is shorter than its diff:
```python
import functools

import jax
import jax.numpy as jnp
from jax import lax
from jax.experimental import pallas as pl
from jax.experimental.pallas import tpu as pltpu
from jax.sharding import PartitionSpec as P

D = 16384
HQ = 64
KVH = 4
HD = 128
STEPS = 4
F32 = jnp.float32
BF16 = jnp.bfloat16
MESH = pl.DeviceIdType.MESH


def m4(v):
    return lax.rem(v + 8, 4)


def place():
    w = lax.axis_index("wide")
    n = lax.axis_index("narrow")
    return w, n, w // 4, lax.rem(w, 4), n // 2, lax.rem(n, 2)


def rcopy(src, dst, ssem, rsem, target):
    return pltpu.make_async_remote_copy(
        src_ref=src,
        dst_ref=dst,
        send_sem=ssem,
        recv_sem=rsem,
        device_id=target,
        device_id_type=MESH,
    )


def greet(w, n):
    barrier = pltpu.get_barrier_semaphore()
    for i in range(1, 8):
        pl.semaphore_signal(
            barrier, inc=1, device_id=(w, lax.rem(n + i, 8)), device_id_type=MESH
        )
    for i in range(1, 16):
        pl.semaphore_signal(
            barrier, inc=1, device_id=(lax.rem(w + i, 16), n), device_id_type=MESH
        )
    pl.semaphore_wait(barrier, 22)


class Copies:
    def __init__(self, ssem, rsem):
        self.ssem, self.rsem, self.sent = ssem, rsem, []

    def send(self, k, src, dst, target):
        c = rcopy(src, dst, self.ssem.at[k], self.rsem.at[k], target)
        c.start()
        self.sent.append(c)

    def take(self, k, dst, target):
        rcopy(dst, dst, self.ssem.at[k], self.rsem.at[k], target).wait_recv()

    def drain(self):
        for c in self.sent:
            c.wait_send()


def gather_half(cp, k0, buf, row0, p1, p2, index, to1, to2):
    full, lo, hi = pl.ds(row0, 32), pl.ds(row0, 16), pl.ds(row0 + 16, 16)

    def at(a, b, rows):
        return buf.at[index(m4(a), m4(b)), rows]

    def send(k, a, b, rows, target):
        r = at(a, b, rows)
        cp.send(k0 + k, r, r, target)

    def take(k, a, b, rows):
        cp.take(k0 + k, at(a, b, rows), to1(1))

    def spread(j, a):
        send(4 + 4 * j, a, p2, full, to2(1))
        send(5 + 4 * j, a, p2, full, to2(-1))

    def onward(j, a):
        take(4 + 4 * j, a, p2 - 1, full)
        send(6 + 4 * j, a, p2 - 1, lo, to2(1))
        take(5 + 4 * j, a, p2 + 1, full)
        send(7 + 4 * j, a, p2 + 1, hi, to2(-1))

    def last(j, a):
        take(6 + 4 * j, a, p2 + 2, lo)
        take(7 + 4 * j, a, p2 + 2, hi)

    def s0():
        send(0, p1, p2, full, to1(1))
        send(1, p1, p2, full, to1(-1))

    def s1():
        spread(0, p1)

    def s2():
        take(0, p1 - 1, p2, full)
        send(2, p1 - 1, p2, lo, to1(1))
        take(1, p1 + 1, p2, full)
        send(3, p1 + 1, p2, hi, to1(-1))
        spread(1, p1 - 1)
        spread(2, p1 + 1)

    def s3():
        onward(0, p1)

    def s4():
        take(2, p1 + 2, p2, lo)
        take(3, p1 + 2, p2, hi)
        spread(3, p1 + 2)

    def s5():
        onward(1, p1 - 1)
        onward(2, p1 + 1)

    def s6():
        last(0, p1)
        onward(3, p1 + 2)

    def s7():
        last(1, p1 - 1)
        last(2, p1 + 1)
        last(3, p1 + 2)

    return [s0, s1, s2, s3, s4, s5, s6, s7]


def project_kernel(
    x_ref, gain_ref, wq_hbm, wkv_hbm, out_ref,
    xs, sq, sqr, buf, wq, wkv, part, pair, ring_o, ring_n, qsend, qrecv,
    wsem, sq_s, sq_r, ag_s, ag_r, rs_s, rs_r, aa_s, aa_r,
):
    w, n, z, x, y, c = place()
    load_q = pltpu.make_async_copy(wq_hbm, wq, wsem.at[0])
    load_kv = pltpu.make_async_copy(wkv_hbm, wkv, wsem.at[1])
    load_q.start()
    load_kv.start()
    acc = jnp.zeros((64, 128), F32)
    for j in range(16):
        cols = slice(j * 128, j * 128 + 128)
        for t in range(4):
            xs[j, pl.ds(t, 16, stride=4), :] = x_ref[t, :, cols].astype(F32)
        acc = acc + xs[j] * xs[j]
    row = jnp.sum(acc, axis=-1, keepdims=True)
    diag = lax.broadcasted_iota(jnp.int32, (64, 128), 0) == lax.broadcasted_iota(
        jnp.int32, (64, 128), 1
    )
    flat = jnp.sum(jnp.where(diag, row, 0.0), axis=0, keepdims=True)
    sq[...] = jnp.broadcast_to(flat, (8, 128))
    greet(w, n)

    sqc = Copies(sq_s, sq_r)
    for i in range(1, 8):
        peer = lax.rem(n + i, 8)
        sqc.send(i - 1, sq, sqr.at[i - 1], (w, peer))
    for i in range(1, 8):
        sqc.take(i - 1, sqr.at[i - 1], (w, n))
    total = sq[...]
    for i in range(7):
        total = total + sqr[i]
    column = jnp.sum(
        jnp.where(diag, jnp.broadcast_to(total[0:1], (64, 128)), 0.0), axis=-1, keepdims=True
    )
    inv = lax.rsqrt(column / D + 1e-05)
    for j in range(16):
        cols = slice(j * 128, j * 128 + 128)
        buf[w, :, cols] = (xs[j] * inv * gain_ref[:, cols].astype(F32)).astype(BF16)

    ag = Copies(ag_s, ag_r)
    first = gather_half(
        ag, 0, buf, 0, x, z, lambda a, b: b * 4 + a,
        lambda d: (z * 4 + m4(x + d), n), lambda d: (m4(z + d) * 4 + x, n),
    )
    second = gather_half(
        ag, 20, buf, 32, z, x, lambda a, b: a * 4 + b,
        lambda d: (m4(z + d) * 4 + x, n), lambda d: (z * 4 + m4(x + d), n),
    )
    for a, b in zip(first, second):
        a()
        b()
    load_q.wait()
    load_kv.wait()

    rs = Copies(rs_s, rs_r)
    other = (w, y * 2 + (1 - c))
    up, down = (w, m4(y + 1) * 2 + c), (w, m4(y - 1) * 2 + c)
    order = (m4(y + 2), m4(y + 1), m4(y - 1), y)

    def project(yy):
        rows = pl.ds(pl.multiple_of(yy * 16, 16), 16)
        lhs = buf[:, rows, :].reshape(256, 2048)
        q = jnp.dot(lhs, wq[...], preferred_element_type=F32).reshape(16, 2, 8, 512)
        kv = jnp.dot(lhs, wkv[...], preferred_element_type=F32).reshape(16, 2, 8, 64)
        for cc in range(2):
            part[cc, yy, :, :, 0:512] = q[:, cc]
            part[cc, yy, :, :, 512:576] = kv[:, cc]

    def step(i, carry):
        yy = m4(y + jnp.where(i == 0, 2, jnp.where(i == 1, 1, jnp.where(i == 2, 3, 0))))
        project(yy)
        rcopy(part.at[1 - c, yy], pair.at[yy], rs_s.at[i], rs_r.at[i], other).start()
        return carry

    lax.fori_loop(0, 4, step, 0)

    def merge(i):
        yy = order[i]
        rcopy(part.at[1 - c, yy], pair.at[yy], rs_s.at[i], rs_r.at[i], other).wait_recv()
        part[c, yy] = part[c, yy] + pair[yy]

    lo, hi = pl.ds(0, 8), pl.ds(8, 8)
    merge(0)
    rs.send(4, part.at[c, order[0], lo], ring_o.at[0], up)
    rs.send(5, part.at[c, order[0], hi], ring_o.at[1], down)
    merge(1)
    rs.send(6, part.at[c, order[1], hi], ring_n.at[0, hi], up)
    merge(2)
    rs.send(7, part.at[c, order[2], lo], ring_n.at[1, lo], down)
    rs.take(4, ring_o.at[0], up)
    part[c, order[1], 0:8] = part[c, order[1], 0:8] + ring_o[0]
    rs.send(8, part.at[c, order[1], lo], ring_n.at[0, lo], up)
    rs.take(5, ring_o.at[1], up)
    part[c, order[2], 8:16] = part[c, order[2], 8:16] + ring_o[1]
    rs.send(9, part.at[c, order[2], hi], ring_n.at[1, hi], down)
    merge(3)
    rs.take(6, ring_n.at[0, hi], up)
    rs.take(7, ring_n.at[1, lo], up)
    rs.take(8, ring_n.at[0, lo], up)
    rs.take(9, ring_n.at[1, hi], up)
    qsend[...] = (part[c, y] + ring_n[0] + ring_n[1]).astype(BF16)

    aa = Copies(aa_s, aa_r)
    for i in range(1, 16):
        peer = lax.rem(w + i, 16)
        aa.send(i - 1, qsend.at[peer], qrecv.at[w], (peer, n))
    qrecv[w] = qsend[w]
    for i in range(1, 16):
        aa.take(i - 1, qrecv.at[lax.rem(w - i + 16, 16)], (w, n))
    out_ref[...] = qrecv[...]
    sqc.drain()
    ag.drain()
    for i in range(4):
        rcopy(
            part.at[1 - c, order[i]], pair.at[order[i]], rs_s.at[i], rs_r.at[i], other
        ).wait_send()
    rs.drain()
    aa.drain()


def project(inputs, norm_gain, w_query, w_keyval):
    dma = pltpu.SemaphoreType.DMA
    vm = pl.BlockSpec(memory_space=pltpu.VMEM)
    return pl.pallas_call(
        project_kernel,
        out_shape=jax.ShapeDtypeStruct((16, 8, 576), BF16),
        in_specs=[vm, vm, pl.BlockSpec(memory_space=pl.ANY), pl.BlockSpec(memory_space=pl.ANY)],
        out_specs=vm,
        scratch_shapes=[
            pltpu.VMEM((16, 64, 128), F32),
            pltpu.VMEM((8, 128), F32),
            pltpu.VMEM((7, 8, 128), F32),
            pltpu.VMEM((16, 64, 2048), BF16),
            pltpu.VMEM((2048, 512), BF16),
            pltpu.VMEM((2048, 64), BF16),
            pltpu.VMEM((2, 4, 16, 8, 576), F32),
            pltpu.VMEM((4, 16, 8, 576), F32),
            pltpu.VMEM((2, 8, 8, 576), F32),
            pltpu.VMEM((2, 16, 8, 576), F32),
            pltpu.VMEM((16, 8, 576), BF16),
            pltpu.VMEM((16, 8, 576), BF16),
            dma((2,)), dma((7,)), dma((7,)), dma((40,)), dma((40,)), dma((10,)), dma((10,)),
            dma((15,)), dma((15,)),
        ],
        compiler_params=pltpu.CompilerParams(
            collective_id=0, has_side_effects=True, vmem_limit_bytes=48 << 20
        ),
        name="project",
    )(inputs, norm_gain.reshape(1, 2048), w_query, w_keyval)


def attend_kernel(len_ref, qkv, cos_ref, sin_ref, k_ref, v_ref, att, nk, nv,
                  qs, kf, vf, sc, os):
    i = pl.program_id(0)
    r, gp = i // 2, lax.rem(i, 2)
    low = lax.broadcasted_iota(jnp.int32, (1, 8, 128), 1) < 4

    @pl.when(i == 0)
    def _():
        cos, sin = cos_ref[...], sin_ref[...]

        def turn(a):
            return (a * cos + pltpu.roll(a, 64, a.ndim - 1) * sin).astype(BF16)

        qs[...] = jnp.zeros_like(qs)
        kf[...] = jnp.zeros_like(kf)
        vf[...] = jnp.zeros_like(vf)
        for p in range(2):
            a = turn(qkv[:, :, p * 256 : p * 256 + 128].astype(F32)).astype(F32)
            b = turn(qkv[:, :, p * 256 + 128 : p * 256 + 256].astype(F32)).astype(F32)
            for rr, tile in (
                (0, jnp.where(low, a, pltpu.roll(b, 4, 1))),
                (1, jnp.where(low, pltpu.roll(a, 4, 1), b)),
            ):
                for g in range(4):
                    gi = g % 2
                    qs[rr, g // 2, gi * 64 + p * 32 : gi * 64 + p * 32 + 32,
                       gi * 128 : gi * 128 + 128] = (
                        tile[4 * g : 4 * g + 4].reshape(32, 128).astype(BF16)
                    )
        for g in range(4):
            key = jnp.concatenate(
                [qkv[2 * g, :, 512:576].astype(F32), qkv[2 * g + 1, :, 512:576].astype(F32)], -1
            )
            val = jnp.concatenate(
                [qkv[2 * g + 8, :, 512:576].astype(F32), qkv[2 * g + 9, :, 512:576].astype(F32)], -1
            )
            kf[0:8, g * 128 : g * 128 + 128] = turn(key)
            vf[0:8, g * 128 : g * 128 + 128] = val.astype(BF16)
        nk[...] = kf[0:8, :]
        nv[...] = vf[0:8, :]

    factor = 1.0 / jnp.sqrt(F32(HD))
    q = qs[r, gp]
    cols = pl.ds(pl.multiple_of(gp * 256, 256), 256)
    length = len_ref[r]
    nt = (((1,), (1,)), ((), ()))

    fs = lax.dot_general(q, kf[:, cols], nt, preferred_element_type=F32) * factor
    lane = lax.broadcasted_iota(jnp.int32, (128, 128), 1)
    step = lax.rem(lax.broadcasted_iota(jnp.int32, (128, 128), 0), 4)
    ok = (lane // 4 == r) & (lane - 4 * r <= step)
    fs = jnp.where(ok, fs, -jnp.inf)

    chunk = 512
    count = 4096 // chunk

    def score(j, top):
        at = pl.ds(pl.multiple_of(j * chunk, chunk), chunk)
        s = lax.dot_general(q, k_ref[0, at, :], nt, preferred_element_type=F32) * factor
        pos = lax.broadcasted_iota(jnp.int32, (128, chunk), 1) + j * chunk
        s = jnp.where(pos < length, s, -jnp.inf)
        sc[:, at] = s
        for u in range(chunk // 128):
            top = jnp.maximum(top, s[:, u * 128 : u * 128 + 128])
        return top

    top = lax.fori_loop(0, count, score, fs)
    top = jnp.max(top, axis=-1, keepdims=True)
    fe = jnp.exp(fs - top)

    def expo(j, acc):
        at = pl.ds(pl.multiple_of(j * chunk, chunk), chunk)
        e = jnp.exp(sc[:, at] - top)
        sc[:, at] = e
        for u in range(chunk // 128):
            acc = acc + e[:, u * 128 : u * 128 + 128]
        return acc

    acc = lax.fori_loop(0, count, expo, fe)
    scale = 1.0 / jnp.sum(acc, axis=-1, keepdims=True)

    def value(j, out):
        at = pl.ds(pl.multiple_of(j * chunk, chunk), chunk)
        p = (sc[:, at] * scale).astype(BF16)
        return out + jnp.dot(p, v_ref[0, at, :], preferred_element_type=F32)

    out = jnp.dot((fe * scale).astype(BF16), vf[:, cols], preferred_element_type=F32)
    out = lax.fori_loop(0, count, value, out)
    os[r, gp, 0] = out[0:64, 0:128]
    os[r, gp, 1] = out[64:128, 128:256]

    @pl.when(i == 3)
    def _():
        for g in range(4):
            for p in range(2):
                rows = slice(p * 32, p * 32 + 32)
                a = os[0, g // 2, g % 2, rows].reshape(4, 8, 128)
                b = os[1, g // 2, g % 2, rows].reshape(4, 8, 128)
                att[4 * g : 4 * g + 4, :, p * 256 : p * 256 + 128] = jnp.where(
                    low, a, pltpu.roll(b, 4, 1)
                ).astype(BF16)
                att[4 * g : 4 * g + 4, :, p * 256 + 128 : p * 256 + 256] = jnp.where(
                    low, pltpu.roll(a, 4, 1), b
                ).astype(BF16)


def attend(qkv, key_cache, value_cache, lengths, positions):
    half = HD // 2
    freq = jnp.exp(
        -jnp.log(F32(500000.0)) * jnp.arange(half, dtype=F32) * 2.0 / (2 * half)
    )
    pos = positions[:, None] + jnp.arange(STEPS, dtype=jnp.int32)[None, :]
    ang = (pos.astype(F32)[..., None] * freq).reshape(8, half)
    cos, sin = jnp.cos(ang), jnp.sin(ang)
    cos2 = jnp.concatenate([cos, cos], -1)
    sin2 = jnp.concatenate([-sin, sin], -1)

    def whole(shape):
        return pl.BlockSpec(shape, lambda i, ln: (0,) * len(shape))

    cache = pl.BlockSpec((1, 4096, 256), lambda i, ln: (i // 2, 0, lax.rem(i, 2)))
    return pl.pallas_call(
        attend_kernel,
        out_shape=(
            jax.ShapeDtypeStruct((16, 8, 512), BF16),
            jax.ShapeDtypeStruct((8, 512), BF16),
            jax.ShapeDtypeStruct((8, 512), BF16),
        ),
        grid_spec=pltpu.PrefetchScalarGridSpec(
            num_scalar_prefetch=1,
            grid=(4,),
            in_specs=[whole((16, 8, 576)), whole((8, 128)), whole((8, 128)), cache, cache],
            out_specs=(whole((16, 8, 512)), whole((8, 512)), whole((8, 512))),
            scratch_shapes=[
                pltpu.VMEM((2, 2, 128, 256), BF16),
                pltpu.VMEM((128, 512), BF16),
                pltpu.VMEM((128, 512), BF16),
                pltpu.VMEM((128, 4096), F32),
                pltpu.VMEM((2, 2, 2, 64, 128), F32),
            ],
        ),
        compiler_params=pltpu.CompilerParams(vmem_limit_bytes=32 << 20),
        name="attend",
    )(lengths, qkv, cos2, sin2, key_cache, value_cache)


def output_kernel(
    att, wo_hbm, out_ref,
    wo, g, gm, prod, so, sn, ro, rn, so2, sn2, ro2, rn2, res,
    wsem, aa_s, aa_r, ag_s, ag_r, st_s, st_r, st2_s, st2_r,
):
    w, n, z, x, y, c = place()
    load = pltpu.make_async_copy(wo_hbm, wo, wsem)
    load.start()
    greet(w, n)

    aa = Copies(aa_s, aa_r)
    for i in range(1, 16):
        peer = lax.rem(w + i, 16)
        aa.send(i - 1, att.at[peer], g.at[n, w], (peer, n))
    g[n, w] = att[w]
    for i in range(1, 16):
        aa.take(i - 1, g.at[n, lax.rem(w - i + 16, 16)], (w, n))

    ag = Copies(ag_s, ag_r)
    other = (w, y * 2 + (1 - c))
    up, down = (w, m4(y + 1) * 2 + c), (w, m4(y - 1) * 2 + c)
    above, below, far = m4(y + 1) * 2 + c, m4(y - 1) * 2 + c, m4(y + 2) * 2 + c
    lo, hi = pl.ds(0, 8), pl.ds(8, 8)
    ag.send(0, g.at[n], g.at[n], up)
    ag.send(1, g.at[n], g.at[n], down)
    ag.send(2, g.at[n], g.at[n], other)
    ag.take(0, g.at[below], up)
    ag.send(3, g.at[below, lo], g.at[below, lo], up)
    ag.send(4, g.at[below], g.at[below], other)
    ag.take(1, g.at[above], up)
    ag.send(5, g.at[above, hi], g.at[above, hi], down)
    ag.send(6, g.at[above], g.at[above], other)
    ag.take(3, g.at[far, lo], up)
    ag.take(5, g.at[far, hi], up)
    ag.send(7, g.at[far], g.at[far], other)
    ag.take(2, g.at[y * 2 + 1 - c], up)
    ag.take(4, g.at[m4(y - 1) * 2 + 1 - c], up)
    ag.take(6, g.at[m4(y + 1) * 2 + 1 - c], up)
    ag.take(7, g.at[m4(y + 2) * 2 + 1 - c], up)

    def regroup(i, carry):
        gm[i] = g[:, i].astype(F32).reshape(64, 512).astype(BF16)
        return carry

    lax.fori_loop(0, 16, regroup, 0)
    load.wait()

    def multiply(i, carry):
        rows = pl.ds(pl.multiple_of((i // 4) * 4, 4), 4)
        cols = pl.ds(pl.multiple_of(lax.rem(i, 4) * 512, 512), 512)
        v = jnp.dot(gm[rows].reshape(256, 512), wo[:, cols], preferred_element_type=F32)
        prod[rows, :, cols] = v.reshape(4, 64, 512)
        return carry

    lax.fori_loop(0, 16, multiply, 0)

    st = Copies(st_s, st_r)
    st2 = Copies(st2_s, st2_r)
    top, bot = pl.ds(0, 32), pl.ds(32, 32)
    halves = (
        (0, x, z, lambda a, b: m4(b) * 4 + m4(a),
         lambda d: (z * 4 + m4(x + d), n), lambda d: (m4(z + d) * 4 + x, n)),
        (1, z, x, lambda a, b: m4(a) * 4 + m4(b),
         lambda d: (m4(z + d) * 4 + x, n), lambda d: (z * 4 + m4(x + d), n)),
    )
    for h, p1, p2, index, to1, to2 in halves:
        cols = pl.ds(h * 1024, 1024)
        for q in range(4):
            so[h, 0, q] = prod[index(p1 + 2, q), top, cols].astype(BF16)
            so[h, 1, q] = prod[index(p1 + 2, q), bot, cols].astype(BF16)
        st.send(h * 6 + 0, so.at[h, 0], ro.at[h, 0], to1(1))
        st.send(h * 6 + 1, so.at[h, 1], ro.at[h, 1], to1(-1))
    for h, p1, p2, index, to1, to2 in halves:
        cols = pl.ds(h * 1024, 1024)
        for q in range(4):
            sn[h, 0, q, bot] = prod[index(p1 + 1, q), bot, cols].astype(BF16)
            sn[h, 1, q, top] = prod[index(p1 - 1, q), top, cols].astype(BF16)
        st.send(h * 6 + 2, sn.at[h, 0, :, bot], rn.at[h, 0, :, bot], to1(1))
        st.send(h * 6 + 3, sn.at[h, 1, :, top], rn.at[h, 1, :, top], to1(-1))
    for h, p1, p2, index, to1, to2 in halves:
        cols = pl.ds(h * 1024, 1024)
        st.take(h * 6 + 0, ro.at[h, 0], to1(1))
        for q in range(4):
            sn[h, 0, q, top] = (
                prod[index(p1 + 1, q), top, cols] + ro[h, 0, q].astype(F32)
            ).astype(BF16)
        st.send(h * 6 + 4, sn.at[h, 0, :, top], rn.at[h, 0, :, top], to1(1))
        st.take(h * 6 + 1, ro.at[h, 1], to1(1))
        for q in range(4):
            sn[h, 1, q, bot] = (
                prod[index(p1 - 1, q), bot, cols] + ro[h, 1, q].astype(F32)
            ).astype(BF16)
        st.send(h * 6 + 5, sn.at[h, 1, :, bot], rn.at[h, 1, :, bot], to1(-1))
    for h, p1, p2, index, to1, to2 in halves:
        cols = pl.ds(h * 1024, 1024)
        st.take(h * 6 + 2, rn.at[h, 0, :, bot], to1(1))
        st.take(h * 6 + 3, rn.at[h, 1, :, top], to1(1))
        st.take(h * 6 + 4, rn.at[h, 0, :, top], to1(1))
        st.take(h * 6 + 5, rn.at[h, 1, :, bot], to1(1))

        def add(b):
            i = index(p1, b)
            b = m4(b)
            prod[i, :, cols] = (
                prod[i, :, cols] + rn[h, 0, b].astype(F32) + rn[h, 1, b].astype(F32)
            )
            return i

        i = add(p2 + 2)
        so2[h, 0] = prod[i, top, cols].astype(BF16)
        so2[h, 1] = prod[i, bot, cols].astype(BF16)
        st2.send(h * 6 + 0, so2.at[h, 0], ro2.at[h, 0], to2(1))
        st2.send(h * 6 + 1, so2.at[h, 1], ro2.at[h, 1], to2(-1))
        i = add(p2 + 1)
        sn2[h, 0, bot] = prod[i, bot, cols].astype(BF16)
        st2.send(h * 6 + 2, sn2.at[h, 0, bot], rn2.at[h, 0, bot], to2(1))
        i = add(p2 - 1)
        sn2[h, 1, top] = prod[i, top, cols].astype(BF16)
        st2.send(h * 6 + 3, sn2.at[h, 1, top], rn2.at[h, 1, top], to2(-1))
        add(p2)
    for h, p1, p2, index, to1, to2 in halves:
        cols = pl.ds(h * 1024, 1024)
        st2.take(h * 6 + 0, ro2.at[h, 0], to1(1))
        sn2[h, 0, top] = (
            prod[index(p1, p2 + 1), top, cols] + ro2[h, 0].astype(F32)
        ).astype(BF16)
        st2.send(h * 6 + 4, sn2.at[h, 0, top], rn2.at[h, 0, top], to2(1))
        st2.take(h * 6 + 1, ro2.at[h, 1], to1(1))
        sn2[h, 1, bot] = (
            prod[index(p1, p2 - 1), bot, cols] + ro2[h, 1].astype(F32)
        ).astype(BF16)
        st2.send(h * 6 + 5, sn2.at[h, 1, bot], rn2.at[h, 1, bot], to2(-1))
    for h, p1, p2, index, to1, to2 in halves:
        cols = pl.ds(h * 1024, 1024)
        st2.take(h * 6 + 2, rn2.at[h, 0, bot], to1(1))
        st2.take(h * 6 + 3, rn2.at[h, 1, top], to1(1))
        st2.take(h * 6 + 4, rn2.at[h, 0, top], to1(1))
        st2.take(h * 6 + 5, rn2.at[h, 1, bot], to1(1))
        for j in range(8):
            sub = slice(j * 128, j * 128 + 128)
            res[h * 8 + j] = (
                prod[w, :, pl.ds(h * 1024 + j * 128, 128)]
                + rn2[h, 0, :, sub].astype(F32)
                + rn2[h, 1, :, sub].astype(F32)
            )
    for j in range(16):
        for t in range(4):
            out_ref[t, :, j * 128 : j * 128 + 128] = res[j, pl.ds(t, 16, stride=4), :].astype(BF16)
    aa.drain()
    ag.drain()
    st.drain()
    st2.drain()


def output(att, w_out):
    dma = pltpu.SemaphoreType.DMA
    vm = pl.BlockSpec(memory_space=pltpu.VMEM)
    return pl.pallas_call(
        output_kernel,
        out_shape=jax.ShapeDtypeStruct((4, 16, 2048), BF16),
        in_specs=[vm, pl.BlockSpec(memory_space=pl.ANY)],
        out_specs=vm,
        scratch_shapes=[
            pltpu.VMEM((512, 2048), BF16),
            pltpu.VMEM((8, 16, 8, 512), BF16),
            pltpu.VMEM((16, 64, 512), BF16),
            pltpu.VMEM((16, 64, 2048), F32),
            pltpu.VMEM((2, 2, 4, 32, 1024), BF16),
            pltpu.VMEM((2, 2, 4, 64, 1024), BF16),
            pltpu.VMEM((2, 2, 4, 32, 1024), BF16),
            pltpu.VMEM((2, 2, 4, 64, 1024), BF16),
            pltpu.VMEM((2, 2, 32, 1024), BF16),
            pltpu.VMEM((2, 2, 64, 1024), BF16),
            pltpu.VMEM((2, 2, 32, 1024), BF16),
            pltpu.VMEM((2, 2, 64, 1024), BF16),
            pltpu.VMEM((16, 64, 128), F32),
            dma, dma((15,)), dma((15,)), dma((8,)), dma((8,)),
            dma((12,)), dma((12,)), dma((12,)), dma((12,)),
        ],
        compiler_params=pltpu.CompilerParams(
            collective_id=1, has_side_effects=True, vmem_limit_bytes=48 << 20
        ),
        name="output",
    )(att, w_out)


def local(inputs, norm_gain, w_query, w_keyval, w_out, key_cache, value_cache, lengths, positions):
    qkv = project(inputs, norm_gain, w_query, w_keyval)
    att, nk, nv = attend(qkv, key_cache, value_cache, lengths, positions)
    attended = output(att, w_out)

    def by_step(a):
        return a.reshape(2, STEPS, KVH * HD).transpose(1, 0, 2)

    return attended, by_step(nk), by_step(nv)


def solution(mesh):
    return jax.shard_map(
        local,
        mesh=mesh,
        in_specs=(
            P(None, "wide", "narrow"),
            P("narrow"),
            P("narrow", "wide"),
            P("narrow", "wide"),
            P("wide", "narrow"),
            P(("wide", "narrow"), None, None),
            P(("wide", "narrow"), None, None),
            P(("wide", "narrow")),
            P(("wide", "narrow")),
        ),
        out_specs=(
            P(None, "wide", "narrow"),
            P(None, ("wide", "narrow"), None),
            P(None, ("wide", "narrow"), None),
        ),
        check_vma=False,
    )
```

time: 842 us -> 144 us (0.17)
  waiting for transfers between devices: 297 us -> 0 us
  other arithmetic: 202 us -> 0.93 us
  Pallas kernels: 0 us -> 128 us
  local copies, waits for them, and re-layouts: 127 us -> 13.9 us
  blocking collectives: 99 us -> 0 us
  matrix products: 63.4 us -> 0 us
  starting transfers between devices: 29 us -> 0 us
  between operations: 15.4 us -> 0.69 us
    unnamed x4 -> x0, other arithmetic: 186 us -> none
    all_gather x4 -> x0, waiting for transfers between devices: 156 us -> none  [local(): shard_piece = lax.all_gather(normed, 'wide', axis=1, tiled=True)]
    pallas_call x0 -> x3, Pallas kernels: none -> 128 us  [the longest x1 58.2 us: project(): pl.pallas_call(project_kernel, out_shape=jax.ShapeDtypeStruct((16, 8, 576...]
    reduce_scatter x8 -> x0, waiting for transfers between devices: 120 us -> none  [the longest x4 68 us: local(): lax.psum_scatter(partials, 'wide', scatter_dimension=1, tiled=True)]
    dot_general x27 -> x0, matrix products: 63.4 us -> none  [the longest x4 23.2 us: local(): jnp.einsum('trgqd,rsgd->rgtqs', grouped, cached, preferred_element_type=j...]
    all_gather x4 -> x0, blocking collectives: 51.7 us -> none  [local(): lax.all_gather(by_heads, 'narrow', axis=2, tiled=True)]
    unnamed x25 -> x14, local copies, waits for them, and re-layouts: 51.4 us -> 11.9 us
    another operation x17 -> x0, local copies, waits for them, and re-layouts: 34.6 us -> none  [the longest x8 27.2 us: local(): attended_heads.reshape(count_steps, 1, rows_dev, HQ * HD)]
  transfers between devices with their start and end apart: 17 -> 0, of which waited for: 10 -> 0; matrix products, arithmetic and copies ran while one was open for 46% -> 0% of each run, Pallas kernels for 0% -> 0%
where the time goes in v1:
time: 144 us; the launch traced here: 143 us
  Pallas kernels  128 us (89%)
  local copies, waits for them, and re-layouts  13.9 us (10%)
    pallas_call x1, Pallas kernels, project(): pl.pallas_call(project_kernel, out_shape=jax.ShapeDtypeStruct((16, 8, 576...  58.2 us
    pallas_call x1, Pallas kernels, output(): pl.pallas_call(output_kernel, out_shape=jax.ShapeDtypeStruct((4, 16, 2048...  50.8 us
    pallas_call x1, Pallas kernels, attend(): pl.pallas_call(attend_kernel, out_shape=(jax.ShapeDtypeStruct((16, 8, 512...  18.8 us
    unnamed x14, local copies, waits for them, and re-layouts  11.9 us

profile of v1, /device:TPU:0, one launch (start us, length us, event | category | flops | bytes accessed | tf_op | source)
XLA Modules:
  0.0 143.4 jit_solution(17985486698341212263)
XLA Ops:
  0.6 0.7 reshape.44.gain_ref
  1.3 1.2 copy.12.wkv_hbm
  2.6 0.0 copy-start.2
  2.6 1.6 %copy-done.2 = bf16[2048,512]{1,0:T(8,128)(2,1)S(1)} copy-done((bf16[2048,512]{1,0:T(8,128)(2,1)S(1)}, bf16[2048,512]{1,0:T(8,128)(2,1)}, u32[]{:S(2)}) %copy-start.2) | copy-done | bytes 2097176
  4.1 0.0 copy-start.4
  4.2 0.9 copy-done.4
  5.1 58.2 %project.1.qkv = bf16[16,8,576]{2,1,0:T(8,128)(2,1)S(1)} custom-call(bf16[4,16,2048]{2,1,0:T(8,128)(2,1)S(1)} %copy-done.4, bf16[1,2048]{1,0:T(2,128)(2,1)S(1)} %reshape.44.gain_ref, bf16[2048,512]{1,0:T(8,128)(2,1)S(1)} %copy-done.2, bf16[2048,64]{1,0:T(8,128)(2,1)S(1)} %copy.12.wkv_hbm), custom_call_target="tpu_custom_call" | custom-call | tf_op jit(solution)/shard_map/project/pallas_call | solution.py:262
  63.3 0.7 add_convert_fusion
  64.1 0.1 convert_element_type.11
  64.1 0.1 fusion
  64.3 0.1 pad_maximum_fusion
  64.3 0.0 copy-start
  64.3 3.4 %copy-done = bf16[2,4096,512]{2,1,0:T(8,128)(2,1)S(1)} copy-done((bf16[2,4096,512]{2,1,0:T(8,128)(2,1)S(1)}, bf16[2,4096,512]{2,1,0:T(8,128)(2,1)}, u32[]{:S(2)}) %copy-start) | copy-done | bytes 8388632
  67.7 0.0 copy-start.1
  67.7 3.4 %copy-done.1 = bf16[2,4096,512]{2,1,0:T(8,128)(2,1)S(1)} copy-done((bf16[2,4096,512]{2,1,0:T(8,128)(2,1)S(1)}, bf16[2,4096,512]{2,1,0:T(8,128)(2,1)}, u32[]{:S(2)}) %copy-start.1) | copy-done | bytes 8388632
  71.1 0.0 copy-start.5
  71.1 0.7 copy-done.5
  71.8 0.0 copy-start.3
  71.8 18.8 %attend.1 = (bf16[16,8,512]{2,1,0:T(8,128)(2,1)S(1)}, bf16[8,512]{1,0:T(8,128)(2,1)S(1)}, bf16[8,512]{1,0:T(8,128)(2,1)S(1)}) custom-call(s32[2]{0:T(128)S(1)} %copy-done.5, bf16[16,8,576]{2,1,0:T(8,128)(2,1)S(1)} %project.1.qkv, f32[8,128]{1,0:T(8,128)S(1)} %get-tuple-element.12.cos_ref, f32[8,128]{1,0:T(8,128)S(1)} %get-tuple-element.13.sin_ref, ...), custom_call_target="tpu_custom_call" | custom-call | tf_op jit(solution)/shard_map/attend/pallas_call | solution.py:411
  90.6 0.0 copy-done.3
  90.6 50.8 %output.1 = bf16[4,16,2048]{2,1,0:T(8,128)(2,1)S(1)} custom-call(bf16[16,8,512]{2,1,0:T(8,128)(2,1)S(1)} %get-tuple-element.6.att, bf16[512,2048]{1,0:T(8,128)(2,1)S(1)} %copy-done.3), custom_call_target="tpu_custom_call" | custom-call | tf_op jit(solution)/shard_map/output/pallas_call | solution.py:593
  141.5 0.6 copy.18
  142.1 0.6 copy.17
  142.7 0.7 copy.20
  (3 shorter events, 0.0 us)
Async XLA Ops:
  2.6 1.6 %copy-start.2 = (bf16[2048,512]{1,0:T(8,128)(2,1)S(1)}, bf16[2048,512]{1,0:T(8,128)(2,1)}, u32[]{:S(2)}) copy-start(bf16[2048,512]{1,0:T(8,128)(2,1)} %wq_hbm.1) | copy-start | bytes 6291460
  4.1 0.9 copy-start.4
  64.3 3.4 %copy-start = (bf16[2,4096,512]{2,1,0:T(8,128)(2,1)S(1)}, bf16[2,4096,512]{2,1,0:T(8,128)(2,1)}, u32[]{:S(2)}) copy-start(bf16[2,4096,512]{2,1,0:T(8,128)(2,1)} %k_ref.1) | copy-start | bytes 25165828
  67.7 3.4 %copy-start.1 = (bf16[2,4096,512]{2,1,0:T(8,128)(2,1)S(1)}, bf16[2,4096,512]{2,1,0:T(8,128)(2,1)}, u32[]{:S(2)}) copy-start(bf16[2,4096,512]{2,1,0:T(8,128)(2,1)} %v_ref.1) | copy-start | bytes 25165828
  71.1 0.7 copy-start.5
  71.8 18.8 %copy-start.3 = (bf16[512,2048]{1,0:T(8,128)(2,1)S(1)}, bf16[512,2048]{1,0:T(8,128)(2,1)}, u32[]{:S(2)}) copy-start(bf16[512,2048]{1,0:T(8,128)(2,1)} %wo_hbm.1) | copy-start | bytes 6291460

commit v2 on v0

v2 whole, which is shorter than its diff:
```python
import jax
import jax.numpy as jnp
from jax import lax
from jax.experimental import pallas as pl
from jax.experimental.pallas import tpu as pltpu
from jax.sharding import PartitionSpec as P

D = 16384
HQ = 64
KVH = 4
HD = 128
STEPS = 4
F32 = jnp.float32
BF16 = jnp.bfloat16
MESH = pl.DeviceIdType.MESH
NT = (((1,), (1,)), ((), ()))
CHUNK = 2048

SLOTS = (
    ((0, 0), (-1, 0), (1, 0), (2, 0)),
    ((-1, -1), (-1, 1), (1, -1), (1, 1)),
    ((0, -1), (0, 1), (2, -1), (2, 1)),
    ((0, 2), (-1, 2), (1, 2), (2, 2)),
)
WHERE = {(a % 4, b % 4): (g, s) for g, row in enumerate(SLOTS) for s, (a, b) in enumerate(row)}
OFFSETS = (2, 1, -1, 0)


def m4(v):
    return lax.rem(v + 8, 4)


def rcopy(src, dst, ssem, rsem, target):
    return pltpu.make_async_remote_copy(
        src_ref=src,
        dst_ref=dst,
        send_sem=ssem,
        recv_sem=rsem,
        device_id=target,
        device_id_type=MESH,
    )


class Copies:
    def __init__(self, ssem, rsem):
        self.ssem, self.rsem, self.sent = ssem, rsem, []

    def send(self, k, src, dst, target):
        c = rcopy(src, dst, self.ssem.at[k], self.rsem.at[k], target)
        c.start()
        self.sent.append(c)

    def take(self, k, dst, target):
        rcopy(dst, dst, self.ssem.at[k], self.rsem.at[k], target).wait_recv()

    def drain(self):
        for c in self.sent:
            c.wait_send()


def gather_half(cp, k0, buf, h, to1, to2):
    full, lo, hi = pl.ds(0, 32), pl.ds(0, 16), pl.ds(16, 16)

    def at(a, b, rows):
        g, s = WHERE[(a % 4, b % 4)]
        return buf.at[g, h, s, rows]

    def send1(k, a, b, rows, d):
        cp.send(k0 + k, at(a, b, rows), at(a - d, b, rows), to1(d))

    def send2(k, a, b, rows, d):
        cp.send(k0 + k, at(a, b, rows), at(a, b - d, rows), to2(d))

    def take(k, a, b, rows):
        cp.take(k0 + k, at(a, b, rows), to1(1))

    def spread(j, a):
        send2(4 + 4 * j, a, 0, full, 1)
        send2(5 + 4 * j, a, 0, full, -1)

    def onward(j, a):
        take(4 + 4 * j, a, -1, full)
        send2(6 + 4 * j, a, -1, lo, 1)
        take(5 + 4 * j, a, 1, full)
        send2(7 + 4 * j, a, 1, hi, -1)

    def last(j, a):
        take(6 + 4 * j, a, 2, lo)
        take(7 + 4 * j, a, 2, hi)

    def s0():
        send1(0, 0, 0, full, 1)
        send1(1, 0, 0, full, -1)

    def s1():
        spread(0, 0)

    def s2():
        take(0, -1, 0, full)
        send1(2, -1, 0, lo, 1)
        take(1, 1, 0, full)
        send1(3, 1, 0, hi, -1)
        spread(1, -1)
        spread(2, 1)

    def s3():
        onward(0, 0)

    def s4():
        take(2, 2, 0, lo)
        take(3, 2, 0, hi)
        spread(3, 2)

    def s5():
        onward(1, -1)
        onward(2, 1)

    def s6():
        last(0, 0)
        onward(3, 2)

    def s7():
        last(1, -1)
        last(2, 1)
        last(3, 2)

    return [s0, s1, s2, s3, s4, s5, s6, s7]


def layer_kernel(
    len_ref, x_hbm, gain_hbm, wq_hbm, wkv_hbm, wo_hbm, k_hbm, v_hbm, cos_ref, sin_ref,
    out_ref, nk, nv,
    xv, gain, wq, wkv, wo, kb, vb,
    xs, sq, sqr, buf, part, pair, ring_o, ring_n, qsend, qrecv,
    qs, kf, vf, sc, os, att, g, gm,
    so, sn, ro, rn, kp, km, so2, sn2, ro2, rn2, res,
    ld, sq_s, sq_r, ag_s, ag_r, ex_s, ex_r, rs_s, rs_r, aa_s, aa_r,
    ao_s, ao_r, gn_s, gn_r, st_s, st_r, st2_s, st2_r,
):
    w = lax.axis_index("wide")
    n = lax.axis_index("narrow")
    z, x, y, c = w // 4, lax.rem(w, 4), n // 2, lax.rem(n, 2)

    def along_x(d):
        return (z * 4 + m4(x + d), n)

    def along_z(d):
        return (m4(z + d) * 4 + x, n)

    other = (w, y * 2 + (1 - c))
    up, down = (w, m4(y + 1) * 2 + c), (w, m4(y - 1) * 2 + c)

    barrier = pltpu.get_barrier_semaphore()
    for i in range(1, 8):
        pl.semaphore_signal(
            barrier, inc=1, device_id=(w, lax.rem(n + i, 8)), device_id_type=MESH
        )
    for d in (1, -1):
        pl.semaphore_signal(barrier, inc=1, device_id=along_x(d), device_id_type=MESH)
        pl.semaphore_signal(barrier, inc=1, device_id=along_z(d), device_id_type=MESH)

    pairs = [(x_hbm, xv), (gain_hbm, gain), (wq_hbm, wq), (wkv_hbm, wkv), (wo_hbm, wo)]
    pairs += [(k_hbm, kb), (v_hbm, vb)]
    loads = [pltpu.make_async_copy(s, d, ld.at[i]) for i, (s, d) in enumerate(pairs)]
    for load in loads[:5]:
        load.start()
    loads[0].wait()
    acc = jnp.zeros((64, 128), F32)
    for j in range(16):
        cols = slice(j * 128, j * 128 + 128)
        for t in range(4):
            xs[j, pl.ds(t, 16, stride=4), :] = xv[t, :, cols].astype(F32)
        acc = acc + xs[j] * xs[j]
    row = jnp.sum(acc, axis=-1, keepdims=True)
    diag = lax.broadcasted_iota(jnp.int32, (64, 128), 0) == lax.broadcasted_iota(
        jnp.int32, (64, 128), 1
    )
    flat = jnp.sum(jnp.where(diag, row, 0.0), axis=0, keepdims=True)
    sq[...] = jnp.broadcast_to(flat, (8, 128))
    pl.semaphore_wait(barrier, 11)

    sqc = Copies(sq_s, sq_r)
    for i in range(1, 8):
        sqc.send(i - 1, sq, sqr.at[i - 1], (w, lax.rem(n + i, 8)))
    loads[5].start()
    loads[6].start()
    for i in range(1, 8):
        sqc.take(i - 1, sqr.at[i - 1], other)
    total = sq[...]
    for i in range(7):
        total = total + sqr[i]
    column = jnp.sum(
        jnp.where(diag, jnp.broadcast_to(total[0:1], (64, 128)), 0.0), axis=-1, keepdims=True
    )
    inv = lax.rsqrt(column / D + 1e-05)
    loads[1].wait()
    for j in range(16):
        cols = slice(j * 128, j * 128 + 128)
        own = (xs[j] * inv * gain[:, cols].astype(F32)).astype(BF16)
        buf[0, 0, 0, :, cols] = own[0:32]
        buf[0, 1, 0, :, cols] = own[32:64]

    ag = Copies(ag_s, ag_r)
    first = gather_half(ag, 0, buf, 0, along_x, along_z)
    second = gather_half(ag, 20, buf, 1, along_z, along_x)

    def gather(*steps):
        for i in steps:
            first[i]()
            second[i]()

    ex, rs, aa = Copies(ex_s, ex_r), Copies(rs_s, rs_r), Copies(aa_s, aa_r)
    far, above, below = m4(y + 2), m4(y + 1), m4(y - 1)

    def multiply(i):
        lhs = buf[i].reshape(256, 2048)
        q = jnp.dot(lhs, wq[...], preferred_element_type=F32)
        kv = lax.dot_general(lhs, wkv[...], NT, preferred_element_type=F32)
        for h in range(2):
            qh = q[h * 128 : h * 128 + 128].reshape(4, 2, 2, 8, 512)
            kvh = kv[h * 128 : h * 128 + 128].reshape(4, 2, 2, 8, 64)
            for yy in range(2):
                for cc in range(2):
                    part[cc, h * 2 + yy, 4 * i : 4 * i + 4, :, 0:512] = qh[:, yy, cc]
                    part[cc, h * 2 + yy, 4 * i : 4 * i + 4, :, 512:576] = kvh[:, yy, cc]
        at = pl.ds(4 * i, 4)
        ex.send(i, part.at[1 - c, :, at], pair.at[:, at], other)

    def ring1(i):
        at, lo, hi = pl.ds(4 * i, 4), pl.ds(4 * i, 2), pl.ds(4 * i + 2, 2)
        ex.take(i, pair.at[:, at], other)
        part[c, :, at] = part[c, :, at] + pair[:, at]
        rs.send(6 * i + 0, part.at[c, far, lo], ring_o.at[0, i], up)
        rs.send(6 * i + 1, part.at[c, far, hi], ring_o.at[1, i], down)
        rs.send(6 * i + 2, part.at[c, above, hi], ring_n.at[0, hi], up)
        rs.send(6 * i + 3, part.at[c, below, lo], ring_n.at[1, lo], down)

    def ring2(i):
        lo, hi = pl.ds(4 * i, 2), pl.ds(4 * i + 2, 2)
        rs.take(6 * i + 0, ring_o.at[0, i], up)
        part[c, above, lo] = part[c, above, lo] + ring_o[0, i]
        rs.send(6 * i + 4, part.at[c, above, lo], ring_n.at[0, lo], up)
        rs.take(6 * i + 1, ring_o.at[1, i], up)
        part[c, below, hi] = part[c, below, hi] + ring_o[1, i]
        rs.send(6 * i + 5, part.at[c, below, hi], ring_n.at[1, hi], down)

    def finish(i):
        at, lo, hi = pl.ds(4 * i, 4), pl.ds(4 * i, 2), pl.ds(4 * i + 2, 2)
        rs.take(6 * i + 2, ring_n.at[0, hi], up)
        rs.take(6 * i + 3, ring_n.at[1, lo], up)
        rs.take(6 * i + 4, ring_n.at[0, lo], up)
        rs.take(6 * i + 5, ring_n.at[1, hi], up)
        qsend[at] = (part[c, y, at] + ring_n[0, at] + ring_n[1, at]).astype(BF16)
        for s, (a, b) in enumerate(SLOTS[i]):
            if (a, b) == (0, 0):
                qrecv[w] = qsend[0]
                continue
            dz, dx = jnp.where(y < 2, b, a), jnp.where(y < 2, a, b)
            k = 4 * i + s
            aa.send(k, qsend.at[k], qrecv.at[w], (m4(z + dz) * 4 + m4(x + dx), n))

    gather(0, 1, 2, 3, 4)
    loads[2].wait()
    loads[3].wait()
    multiply(0)
    gather(5)
    multiply(1)
    ring1(0)
    gather(6)
    multiply(2)
    ring1(1)
    ring2(0)
    gather(7)
    multiply(3)
    finish(0)
    ring1(2)
    ring2(1)
    ring1(3)
    ring2(2)
    finish(1)
    ring2(3)
    finish(2)
    finish(3)
    for i in range(4):
        for s, (a, b) in enumerate(SLOTS[i]):
            if (a, b) != (0, 0):
                dz, dx = jnp.where(y < 2, b, a), jnp.where(y < 2, a, b)
                source = m4(z - dz) * 4 + m4(x - dx)
                aa.take(4 * i + s, qrecv.at[source], other)

    low = lax.broadcasted_iota(jnp.int32, (1, 8, 128), 1) < 4
    cos, sin = cos_ref[...], sin_ref[...]

    def turn(a):
        return (a * cos + pltpu.roll(a, 64, a.ndim - 1) * sin).astype(BF16)

    qs[...] = jnp.zeros_like(qs)
    kf[...] = jnp.zeros_like(kf)
    vf[...] = jnp.zeros_like(vf)
    for p in range(2):
        a = turn(qrecv[:, :, p * 256 : p * 256 + 128].astype(F32)).astype(F32)
        b = turn(qrecv[:, :, p * 256 + 128 : p * 256 + 256].astype(F32)).astype(F32)
        for rr, tile in (
            (0, jnp.where(low, a, pltpu.roll(b, 4, 1))),
            (1, jnp.where(low, pltpu.roll(a, 4, 1), b)),
        ):
            for h in range(4):
                gi = h % 2
                qs[rr, h // 2, gi * 64 + p * 32 : gi * 64 + p * 32 + 32,
                   gi * 128 : gi * 128 + 128] = (
                    tile[4 * h : 4 * h + 4].reshape(32, 128).astype(BF16)
                )
    for h in range(4):
        key = jnp.concatenate(
            [qrecv[2 * h, :, 512:576].astype(F32), qrecv[2 * h + 1, :, 512:576].astype(F32)], -1
        )
        val = jnp.concatenate(
            [qrecv[2 * h + 8, :, 512:576].astype(F32), qrecv[2 * h + 9, :, 512:576].astype(F32)], -1
        )
        kf[0:8, h * 128 : h * 128 + 128] = turn(key)
        vf[0:8, h * 128 : h * 128 + 128] = val.astype(BF16)
    nk[...] = kf[0:8, :]
    nv[...] = vf[0:8, :]
    loads[5].wait()
    loads[6].wait()

    factor = 1.0 / jnp.sqrt(F32(HD))
    lane = lax.broadcasted_iota(jnp.int32, (128, 128), 1)
    step = lax.rem(lax.broadcasted_iota(jnp.int32, (128, 128), 0), 4)
    place = lax.broadcasted_iota(jnp.int32, (128, CHUNK), 1)

    def attend(i, carry):
        r, gp = lax.rem(i, 2), i // 2
        q = qs[r, gp]
        cols = pl.ds(pl.multiple_of(gp * 256, 256), 256)
        length = len_ref[r]
        fs = lax.dot_general(q, kf[:, cols], NT, preferred_element_type=F32) * factor
        fs = jnp.where((lane // 4 == r) & (lane - 4 * r <= step), fs, -jnp.inf)

        def score(j, top):
            at = pl.ds(pl.multiple_of(j * CHUNK, CHUNK), CHUNK)
            s = lax.dot_general(q, kb[r, at, cols], NT, preferred_element_type=F32) * factor
            s = jnp.where(place < length - j * CHUNK, s, -jnp.inf)
            sc[:, at] = s
            for u in range(CHUNK // 128):
                top = jnp.maximum(top, s[:, u * 128 : u * 128 + 128])
            return top

        top = lax.fori_loop(0, 4096 // CHUNK, score, fs)
        top = jnp.max(top, axis=-1, keepdims=True)
        fe = jnp.exp(fs - top)

        def expo(j, acc):
            at = pl.ds(pl.multiple_of(j * CHUNK, CHUNK), CHUNK)
            e = jnp.exp(sc[:, at] - top)
            sc[:, at] = e
            for u in range(CHUNK // 128):
                acc = acc + e[:, u * 128 : u * 128 + 128]
            return acc

        acc = lax.fori_loop(0, 4096 // CHUNK, expo, fe)
        scale = 1.0 / jnp.sum(acc, axis=-1, keepdims=True)

        def value(j, out):
            at = pl.ds(pl.multiple_of(j * CHUNK, CHUNK), CHUNK)
            p = (sc[:, at] * scale).astype(BF16)
            return out + jnp.dot(p, vb[r, at, cols], preferred_element_type=F32)

        out = jnp.dot((fe * scale).astype(BF16), vf[:, cols], preferred_element_type=F32)
        out = lax.fori_loop(0, 4096 // CHUNK, value, out)
        os[r, gp, 0] = out[0:64, 0:128]
        os[r, gp, 1] = out[64:128, 128:256]
        return carry

    lax.fori_loop(0, 4, attend, 0)
    for h in range(4):
        for p in range(2):
            rows = slice(p * 32, p * 32 + 32)
            a = os[0, h // 2, h % 2, rows].reshape(4, 8, 128)
            b = os[1, h // 2, h % 2, rows].reshape(4, 8, 128)
            att[4 * h : 4 * h + 4, :, p * 256 : p * 256 + 128] = jnp.where(
                low, a, pltpu.roll(b, 4, 1)
            ).astype(BF16)
            att[4 * h : 4 * h + 4, :, p * 256 + 128 : p * 256 + 256] = jnp.where(
                low, pltpu.roll(a, 4, 1), b
            ).astype(BF16)

    ao = Copies(ao_s, ao_r)
    for i in range(1, 16):
        peer = lax.rem(w + i, 16)
        ao.send(i - 1, att.at[peer], g.at[n, w], (peer, n))
    g[n, w] = att[w]
    for i in range(1, 16):
        ao.take(i - 1, g.at[n, lax.rem(w - i + 16, 16)], other)

    gn = Copies(gn_s, gn_r)
    na, nb, nf = above * 2 + c, below * 2 + c, far * 2 + c
    lo, hi = pl.ds(0, 8), pl.ds(8, 8)
    gn.send(0, g.at[n], g.at[n], up)
    gn.send(1, g.at[n], g.at[n], down)
    gn.send(2, g.at[n], g.at[n], other)
    gn.take(0, g.at[nb], up)
    gn.send(3, g.at[nb, lo], g.at[nb, lo], up)
    gn.send(4, g.at[nb], g.at[nb], other)
    gn.take(1, g.at[na], up)
    gn.send(5, g.at[na, hi], g.at[na, hi], down)
    gn.send(6, g.at[na], g.at[na], other)
    gn.take(3, g.at[nf, lo], up)
    gn.take(5, g.at[nf, hi], up)
    gn.send(7, g.at[nf], g.at[nf], other)
    gn.take(2, g.at[y * 2 + 1 - c], up)
    gn.take(4, g.at[below * 2 + 1 - c], up)
    gn.take(6, g.at[above * 2 + 1 - c], up)
    gn.take(7, g.at[far * 2 + 1 - c], up)

    def regroup(i, carry):
        gm[i] = g[:, i].astype(F32).reshape(64, 512).astype(BF16)
        return carry

    lax.fori_loop(0, 16, regroup, 0)
    loads[4].wait()

    st, st2 = Copies(st_s, st_r), Copies(st2_s, st2_r)
    halves = (
        (0, lambda a, b: m4(z + b) * 4 + m4(x + a), along_x, along_z),
        (1, lambda a, b: m4(z + a) * 4 + m4(x + b), along_z, along_x),
    )
    top, bot = pl.ds(0, 32), pl.ds(32, 32)

    def product(h, index, a):
        lhs = jnp.concatenate([gm[index(a, b)] for b in OFFSETS], axis=0)
        cols = slice(h * 1024, h * 1024 + 1024)
        v = jnp.dot(lhs, wo[:, cols], preferred_element_type=F32)
        return v.reshape(4, 64, 1024)

    for h, index, to1, to2 in halves:
        v = product(h, index, 2)
        so[h, 0] = v[:, 0:32].astype(BF16)
        so[h, 1] = v[:, 32:64].astype(BF16)
        for q in range(4):
            st.send(h * 24 + q, so.at[h, 0, q], ro.at[h, 0, q], to1(1))
            st.send(h * 24 + 4 + q, so.at[h, 1, q], ro.at[h, 1, q], to1(-1))
    for h, index, to1, to2 in halves:
        v = product(h, index, 1)
        sn[h, 0, :, 32:64] = v[:, 32:64].astype(BF16)
        kp[h, 0] = v[:, 0:32]
        for q in range(4):
            st.send(h * 24 + 8 + q, sn.at[h, 0, q, bot], rn.at[h, 0, q, bot], to1(1))
        v = product(h, index, -1)
        sn[h, 1, :, 0:32] = v[:, 0:32].astype(BF16)
        kp[h, 1] = v[:, 32:64]
        for q in range(4):
            st.send(h * 24 + 12 + q, sn.at[h, 1, q, top], rn.at[h, 1, q, top], to1(-1))
    for h, index, to1, to2 in halves:
        km[h] = product(h, index, 0)
    for q in range(4):
        for h, index, to1, to2 in halves:
            st.take(h * 24 + q, ro.at[h, 0, q], to1(1))
            sn[h, 0, q, 0:32] = (kp[h, 0, q] + ro[h, 0, q].astype(F32)).astype(BF16)
            st.send(h * 24 + 16 + q, sn.at[h, 0, q, top], rn.at[h, 0, q, top], to1(1))
            st.take(h * 24 + 4 + q, ro.at[h, 1, q], to1(1))
            sn[h, 1, q, 32:64] = (kp[h, 1, q] + ro[h, 1, q].astype(F32)).astype(BF16)
            st.send(h * 24 + 20 + q, sn.at[h, 1, q, bot], rn.at[h, 1, q, bot], to1(-1))
    for q in range(4):
        for h, index, to1, to2 in halves:
            st.take(h * 24 + 8 + q, rn.at[h, 0, q, bot], to1(1))
            st.take(h * 24 + 12 + q, rn.at[h, 1, q, top], to1(1))
            st.take(h * 24 + 16 + q, rn.at[h, 0, q, top], to1(1))
            st.take(h * 24 + 20 + q, rn.at[h, 1, q, bot], to1(1))
            v = km[h, q] + rn[h, 0, q].astype(F32) + rn[h, 1, q].astype(F32)
            if q == 0:
                so2[h] = v.reshape(2, 32, 1024).astype(BF16)
                st2.send(h * 6 + 0, so2.at[h, 0], ro2.at[h, 0], to2(1))
                st2.send(h * 6 + 1, so2.at[h, 1], ro2.at[h, 1], to2(-1))
            elif q == 1:
                sn2[h, 0, 32:64] = v[32:64].astype(BF16)
                km[h, q] = v
                st2.send(h * 6 + 2, sn2.at[h, 0, bot], rn2.at[h, 0, bot], to2(1))
            elif q == 2:
                sn2[h, 1, 0:32] = v[0:32].astype(BF16)
                km[h, q] = v
                st2.send(h * 6 + 3, sn2.at[h, 1, top], rn2.at[h, 1, top], to2(-1))
            else:
                km[h, q] = v
        if q == 2:
            for h, index, to1, to2 in halves:
                st2.take(h * 6 + 0, ro2.at[h, 0], to1(1))
                sn2[h, 0, 0:32] = (km[h, 1, 0:32] + ro2[h, 0].astype(F32)).astype(BF16)
                st2.send(h * 6 + 4, sn2.at[h, 0, top], rn2.at[h, 0, top], to2(1))
                st2.take(h * 6 + 1, ro2.at[h, 1], to1(1))
                sn2[h, 1, 32:64] = (km[h, 2, 32:64] + ro2[h, 1].astype(F32)).astype(BF16)
                st2.send(h * 6 + 5, sn2.at[h, 1, bot], rn2.at[h, 1, bot], to2(-1))
    for h, index, to1, to2 in halves:
        st2.take(h * 6 + 2, rn2.at[h, 0, bot], to1(1))
        st2.take(h * 6 + 3, rn2.at[h, 1, top], to1(1))
        st2.take(h * 6 + 4, rn2.at[h, 0, top], to1(1))
        st2.take(h * 6 + 5, rn2.at[h, 1, bot], to1(1))
        for j in range(8):
            sub = slice(j * 128, j * 128 + 128)
            res[h * 8 + j] = (
                km[h, 3, :, sub] + rn2[h, 0, :, sub].astype(F32) + rn2[h, 1, :, sub].astype(F32)
            )
    for j in range(16):
        for t in range(4):
            out_ref[t, :, j * 128 : j * 128 + 128] = res[j, pl.ds(t, 16, stride=4), :].astype(BF16)
    for group in (sqc, ag, ex, rs, aa, ao, gn, st, st2):
        group.drain()


def local(inputs, norm_gain, w_query, w_keyval, w_out, key_cache, value_cache, lengths, positions):
    half = HD // 2
    freq = jnp.exp(-jnp.log(F32(500000.0)) * jnp.arange(half, dtype=F32) * 2.0 / (2 * half))
    pos = positions[:, None] + jnp.arange(STEPS, dtype=jnp.int32)[None, :]
    ang = (pos.astype(F32)[..., None] * freq).reshape(8, half)
    cos, sin = jnp.cos(ang), jnp.sin(ang)
    cos2 = jnp.concatenate([cos, cos], -1)
    sin2 = jnp.concatenate([-sin, sin], -1)

    dma = pltpu.SemaphoreType.DMA
    vm = pl.BlockSpec(memory_space=pltpu.VMEM)
    hbm = pl.BlockSpec(memory_space=pl.ANY)

    def b16(*shape):
        return pltpu.VMEM(shape, BF16)

    def f32(*shape):
        return pltpu.VMEM(shape, F32)

    attended, nk, nv = pl.pallas_call(
        layer_kernel,
        out_shape=(
            jax.ShapeDtypeStruct((4, 16, 2048), BF16),
            jax.ShapeDtypeStruct((8, 512), BF16),
            jax.ShapeDtypeStruct((8, 512), BF16),
        ),
        in_specs=[pl.BlockSpec(memory_space=pltpu.SMEM)] + [hbm] * 7 + [vm, vm],
        out_specs=(vm, vm, vm),
        scratch_shapes=[
            b16(4, 16, 2048), b16(1, 2048), b16(2048, 512), b16(64, 2048), b16(512, 2048),
            b16(2, 4096, 512), b16(2, 4096, 512),
            f32(16, 64, 128), f32(8, 128), f32(7, 8, 128), b16(4, 2, 4, 32, 2048),
            f32(2, 4, 16, 8, 576), f32(4, 16, 8, 576), f32(2, 4, 2, 8, 576),
            f32(2, 16, 8, 576), b16(16, 8, 576), b16(16, 8, 576),
            b16(2, 2, 128, 256), b16(128, 512), b16(128, 512), f32(128, 4096),
            f32(2, 2, 2, 64, 128), b16(16, 8, 512), b16(8, 16, 8, 512), b16(16, 64, 512),
            b16(2, 2, 4, 32, 1024), b16(2, 2, 4, 64, 1024),
            b16(2, 2, 4, 32, 1024), b16(2, 2, 4, 64, 1024),
            f32(2, 2, 4, 32, 1024), f32(2, 4, 64, 1024),
            b16(2, 2, 32, 1024), b16(2, 2, 64, 1024), b16(2, 2, 32, 1024), b16(2, 2, 64, 1024),
            f32(16, 64, 128),
            dma((7,)), dma((7,)), dma((7,)), dma((40,)), dma((40,)), dma((4,)), dma((4,)),
            dma((24,)), dma((24,)), dma((16,)), dma((16,)), dma((15,)), dma((15,)),
            dma((8,)), dma((8,)), dma((48,)), dma((48,)), dma((12,)), dma((12,)),
        ],
        compiler_params=pltpu.CompilerParams(
            collective_id=0, has_side_effects=True, vmem_limit_bytes=60 << 20
        ),
        name="layer",
    )(
        lengths, inputs, norm_gain.reshape(1, 2048), w_query, w_keyval.T, w_out,
        key_cache, value_cache, cos2, sin2,
    )

    def by_step(a):
        return a.reshape(2, STEPS, KVH * HD).transpose(1, 0, 2)

    return attended, by_step(nk), by_step(nv)


def solution(mesh):
    return jax.shard_map(
        local,
        mesh=mesh,
        in_specs=(
            P(None, "wide", "narrow"),
            P("narrow"),
            P("narrow", "wide"),
            P("narrow", "wide"),
            P("wide", "narrow"),
            P(("wide", "narrow"), None, None),
            P(("wide", "narrow"), None, None),
            P(("wide", "narrow")),
            P(("wide", "narrow")),
        ),
        out_specs=(
            P(None, "wide", "narrow"),
            P(None, ("wide", "narrow"), None),
            P(None, ("wide", "narrow"), None),
        ),
        check_vma=False,
    )
```

time: 842 us -> 114 us (0.14)
  waiting for transfers between devices: 297 us -> 0 us
  other arithmetic: 202 us -> 1.52 us
  local copies, waits for them, and re-layouts: 127 us -> 5.67 us
  Pallas kernels: 0 us -> 104 us
  blocking collectives: 99 us -> 0 us
  matrix products: 63.4 us -> 0 us
  starting transfers between devices: 29 us -> 0 us
  between operations: 15.4 us -> 0.65 us
    unnamed x4 -> x0, other arithmetic: 186 us -> none
    all_gather x4 -> x0, waiting for transfers between devices: 156 us -> none  [local(): shard_piece = lax.all_gather(normed, 'wide', axis=1, tiled=True)]
    reduce_scatter x8 -> x0, waiting for transfers between devices: 120 us -> none  [the longest x4 68 us: local(): lax.psum_scatter(partials, 'wide', scatter_dimension=1, tiled=True)]
    pallas_call x0 -> x1, Pallas kernels: none -> 104 us  [local(): pl.pallas_call(layer_kernel, out_shape=(jax.ShapeDtypeStruct((4, 16, 2048...]
    dot_general x27 -> x0, matrix products: 63.4 us -> none  [the longest x4 23.2 us: local(): jnp.einsum('trgqd,rsgd->rgtqs', grouped, cached, preferred_element_type=j...]
    all_gather x4 -> x0, blocking collectives: 51.7 us -> none  [local(): lax.all_gather(by_heads, 'narrow', axis=2, tiled=True)]
    unnamed x25 -> x1, local copies, waits for them, and re-layouts: 51.4 us -> 1.67 us
    another operation x17 -> x0, local copies, waits for them, and re-layouts: 34.6 us -> none  [the longest x8 27.2 us: local(): attended_heads.reshape(count_steps, 1, rows_dev, HQ * HD)]
  transfers between devices with their start and end apart: 17 -> 0, of which waited for: 10 -> 0; matrix products, arithmetic and copies ran while one was open for 46% -> 0% of each run, Pallas kernels for 0% -> 0%
where the time goes in v2:
time: 114 us; the launch traced here: 112 us
  Pallas kernels  104 us (91%)
  local copies, waits for them, and re-layouts  5.67 us (5%)
  other arithmetic  1.52 us (1%)
    pallas_call x1, Pallas kernels, local(): pl.pallas_call(layer_kernel, out_shape=(jax.ShapeDtypeStruct((4, 16, 2048...  104 us
    reshape x4, local copies, waits for them, and re-layouts, by_step(): return a.reshape(2, STEPS, KVH * HD).transpose(1, 0, 2)  2.63 us

profile of v2, /device:TPU:0, one launch (start us, length us, event | category | flops | bytes accessed | tf_op | source)
XLA Modules:
  0.0 112.1 jit_solution(219148884593422219)
XLA Ops:
  0.6 0.7 add_convert_fusion
  1.4 0.1 convert_element_type.11
  1.5 1.3 %reshape.44.gain_hbm = bf16[1,2048]{1,0:T(2,128)(2,1)} reshape(bf16[2048]{0:T(1024)(128)(2,1)} %param.10) | data formatting | bytes 8192 | tf_op jit(solution)/shard_map/reshape | solution.py:560
  2.7 0.1 fusion
  2.9 0.7 pad_maximum_fusion
  3.5 104.3 %layer.1 = (bf16[4,16,2048]{2,1,0:T(8,128)(2,1)}, bf16[8,512]{1,0:T(8,128)(2,1)}, bf16[8,512]{1,0:T(8,128)(2,1)}) custom-call(s32[2]{0:T(128)} %len_ref.1, bf16[4,16,2048]{2,1,0:T(8,128)(2,1)} %x_hbm.1, bf16[1,2048]{1,0:T(2,128)(2,1)} %reshape.44.gain_hbm, bf16[2048,512]{1,0:T(8,128)(2,1)} %wq_hbm.1, bf16[64,2048]{1,0:T(8,128)(2,1)} %bitcast.7, ...), custom_call_target="tpu_custom_call" | custom-call | tf_op jit(solution)/shard_map/layer/pallas_call | solution.py:529
  107.8 0.7 reshape.45
  108.5 0.6 copy.17
  109.1 0.7 reshape.46
  109.8 0.6 copy.16
  110.4 1.7 %copy.19 = bf16[4,16,2048]{2,1,0:T(8,128)(2,1)} copy(bf16[4,16,2048]{2,1,0:T(8,128)(2,1)} %get-tuple-element.17) | data formatting | bytes 524288
  (1 shorter events, 0.0 us)

commit v3 on v2

v3 whole, which is shorter than its diff:
```python
import jax
import jax.numpy as jnp
import numpy as np
from jax import lax
from jax.experimental import pallas as pl
from jax.experimental.pallas import tpu as pltpu
from jax.sharding import PartitionSpec as P

D = 16384
HQ = 64
KVH = 4
HD = 128
STEPS = 4
F32 = jnp.float32
BF16 = jnp.bfloat16
MESH = pl.DeviceIdType.MESH
NT = (((1,), (1,)), ((), ()))
CHUNK = 2048

SLOTS = (
    ((0, 0), (-1, 0), (1, 0), (2, 0)),
    ((-1, -1), (-1, 1), (1, -1), (1, 1)),
    ((0, -1), (0, 1), (2, -1), (2, 1)),
    ((0, 2), (-1, 2), (1, 2), (2, 2)),
)
WHERE = {(a % 4, b % 4): (g, s) for g, row in enumerate(SLOTS) for s, (a, b) in enumerate(row)}
OFFSETS = (2, 1, -1, 0)
FREQ = np.exp(
    -np.log(np.float32(500000.0)) * np.arange(64, dtype=np.float32) * np.float32(2.0) / np.float32(128)
)


def m4(v):
    return lax.rem(v + 8, 4)


def rcopy(src, dst, ssem, rsem, target):
    return pltpu.make_async_remote_copy(
        src_ref=src,
        dst_ref=dst,
        send_sem=ssem,
        recv_sem=rsem,
        device_id=target,
        device_id_type=MESH,
    )


class Copies:
    def __init__(self, ssem, rsem):
        self.ssem, self.rsem, self.sent = ssem, rsem, []

    def send(self, k, src, dst, target):
        c = rcopy(src, dst, self.ssem.at[k], self.rsem.at[k], target)
        c.start()
        self.sent.append(c)

    def take(self, k, dst, target):
        rcopy(dst, dst, self.ssem.at[k], self.rsem.at[k], target).wait_recv()

    def drain(self):
        for c in self.sent:
            c.wait_send()


def gather_half(cp, k0, buf, r, h, to1, to2):
    full, lo, hi = pl.ds(0, 2048), pl.ds(0, 1024), pl.ds(1024, 1024)

    def at(a, b, cols):
        g, s = WHERE[(a % 4, b % 4)]
        return buf.at[r, g, h, s, :, cols]

    def send1(k, a, b, cols, d):
        cp.send(k0 + k, at(a, b, cols), at(a - d, b, cols), to1(d))

    def send2(k, a, b, cols, d):
        cp.send(k0 + k, at(a, b, cols), at(a, b - d, cols), to2(d))

    def take(k, a, b, cols):
        cp.take(k0 + k, at(a, b, cols), to1(1))

    def spread(j, a):
        send2(4 + 4 * j, a, 0, full, 1)
        send2(5 + 4 * j, a, 0, full, -1)

    def onward(j, a):
        take(4 + 4 * j, a, -1, full)
        send2(6 + 4 * j, a, -1, lo, 1)
        take(5 + 4 * j, a, 1, full)
        send2(7 + 4 * j, a, 1, hi, -1)

    def last(j, a):
        take(6 + 4 * j, a, 2, lo)
        take(7 + 4 * j, a, 2, hi)

    def s0():
        send1(0, 0, 0, full, 1)
        send1(1, 0, 0, full, -1)

    def s1():
        spread(0, 0)

    def s2():
        take(0, -1, 0, full)
        send1(2, -1, 0, lo, 1)
        take(1, 1, 0, full)
        send1(3, 1, 0, hi, -1)
        spread(1, -1)
        spread(2, 1)

    def s3():
        onward(0, 0)

    def s4():
        take(2, 2, 0, lo)
        take(3, 2, 0, hi)
        spread(3, 2)

    def s5():
        onward(1, -1)
        onward(2, 1)

    def s6():
        last(0, 0)
        onward(3, 2)

    def s7():
        last(1, -1)
        last(2, 1)
        last(3, 2)

    return [s0, s1, s2, s3, s4, s5, s6, s7]


def zip_rows(a, b):
    low = lax.broadcasted_iota(jnp.int32, (1,) * (a.ndim - 2) + (8, a.shape[-1]), a.ndim - 2) < 4
    axis = a.ndim - 2
    return (
        jnp.where(low, a, pltpu.roll(b, 4, axis)),
        jnp.where(low, pltpu.roll(a, 4, axis), b),
    )


def layer_kernel(
    len_ref, pos_ref, x_hbm, gain_hbm, wq_hbm, wkv_hbm, wo_hbm, k_hbm, v_hbm,
    out_ref, nk, nv,
    xv, gain, wq, wkv, wo, kb, vb,
    xs, sq, sqr, buf, part, pair, ring_o, ring_n, qsend, qrecv, qx,
    qs, kf, vf, kvout, sc, att, g, gm,
    so, sn, ro, rn, kp, km, so2, sn2, ro2, rn2, res, rows16,
    ld, sq_s, sq_r, ag_s, ag_r, ex_s, ex_r, rs_s, rs_r, aa_s, aa_r,
    ao_s, ao_r, gn_s, gn_r, st_s, st_r, st2_s, st2_r,
):
    w = lax.axis_index("wide")
    n = lax.axis_index("narrow")
    z, x, y, c = w // 4, lax.rem(w, 4), n // 2, lax.rem(n, 2)

    def along_x(d):
        return (z * 4 + m4(x + d), n)

    def along_z(d):
        return (m4(z + d) * 4 + x, n)

    other = (w, y * 2 + (1 - c))
    up, down = (w, m4(y + 1) * 2 + c), (w, m4(y - 1) * 2 + c)
    far, above, below = m4(y + 2), m4(y + 1), m4(y - 1)

    barrier = pltpu.get_barrier_semaphore()
    for i in range(1, 8):
        pl.semaphore_signal(
            barrier, inc=1, device_id=(w, lax.rem(n + i, 8)), device_id_type=MESH
        )
    for d in (1, -1):
        pl.semaphore_signal(barrier, inc=1, device_id=along_x(d), device_id_type=MESH)
        pl.semaphore_signal(barrier, inc=1, device_id=along_z(d), device_id_type=MESH)

    pairs = [(x_hbm, xv), (gain_hbm, gain), (wq_hbm, wq), (wkv_hbm, wkv), (wo_hbm, wo)]
    pairs += [(k_hbm, kb), (v_hbm, vb)]
    loads = [pltpu.make_async_copy(s, d, ld.at[i]) for i, (s, d) in enumerate(pairs)]
    for load in loads[:5]:
        load.start()
    qs[...] = jnp.zeros_like(qs)
    kf[...] = jnp.zeros_like(kf)
    vf[...] = jnp.zeros_like(vf)
    loads[0].wait()
    acc = jnp.zeros((64, 128), F32)
    for j in range(16):
        cols = slice(j * 128, j * 128 + 128)
        for t in range(4):
            xs[j, pl.ds(t, 16, stride=4), :] = xv[t, :, cols].astype(F32)
        acc = acc + xs[j] * xs[j]
    row = jnp.sum(acc, axis=-1, keepdims=True)
    diag = lax.broadcasted_iota(jnp.int32, (64, 128), 0) == lax.broadcasted_iota(
        jnp.int32, (64, 128), 1
    )
    flat = jnp.sum(jnp.where(diag, row, 0.0), axis=0, keepdims=True)
    sq[...] = jnp.broadcast_to(flat, (8, 128))
    pl.semaphore_wait(barrier, 11)

    sqc = Copies(sq_s, sq_r)
    for i in range(1, 8):
        sqc.send(i - 1, sq, sqr.at[i - 1], (w, lax.rem(n + i, 8)))
    loads[5].start()
    loads[6].start()

    spot = lax.rem(lax.broadcasted_iota(jnp.int32, (8, 128), 1), 64)
    freq = jnp.zeros((8, 128), F32)
    for i in range(64):
        freq = jnp.where(spot == i, F32(FREQ[i]), freq)
    later = lax.rem(lax.broadcasted_iota(jnp.int32, (8, 128), 0), 4)
    left = lax.broadcasted_iota(jnp.int32, (8, 128), 1) < 64
    turns = []
    for r in range(2):
        angle = (later + pos_ref[r]).astype(F32) * freq
        sine = jnp.sin(angle)
        turns.append((jnp.cos(angle), jnp.where(left, -sine, sine)))

    for i in range(1, 8):
        sqc.take(i - 1, sqr.at[i - 1], other)
    total = sq[...]
    for i in range(7):
        total = total + sqr[i]
    column = jnp.sum(
        jnp.where(diag, jnp.broadcast_to(total[0:1], (64, 128)), 0.0), axis=-1, keepdims=True
    )
    inv = lax.rsqrt(column / D + 1e-05)
    loads[1].wait()
    for j in range(16):
        cols = slice(j * 128, j * 128 + 128)
        own = (xs[j] * inv * gain[cols].astype(F32).reshape(1, 128)).reshape(4, 2, 8, 128)
        for r, v in enumerate(zip_rows(own[:, 0], own[:, 1])):
            v = v.reshape(32, 128).astype(BF16)
            buf[r, 0, 0, 0, :, cols] = v[0:16]
            buf[r, 0, 1, 0, :, cols] = v[16:32]

    ag = Copies(ag_s, ag_r)
    ways = [
        [
            gather_half(ag, r * 40, buf, r, 0, along_x, along_z),
            gather_half(ag, r * 40 + 20, buf, r, 1, along_z, along_x),
        ]
        for r in range(2)
    ]

    def gather(r, *steps):
        for i in steps:
            ways[r][0][i]()
            ways[r][1][i]()

    ex, rs, aa = Copies(ex_s, ex_r), Copies(rs_s, rs_r), Copies(aa_s, aa_r)

    def multiply(r, m):
        lhs = buf[r, 2 * m : 2 * m + 2].reshape(256, 2048)
        q = jnp.dot(lhs, wq[...], preferred_element_type=F32)
        kv = lax.dot_general(lhs, wkv[...], NT, preferred_element_type=F32)
        for cols, v in ((slice(0, 512), q), (slice(512, 576), kv)):
            v = v.reshape(2, 2, 2, 2, 2, 8, v.shape[-1])
            for h in range(2):
                for yy in range(2):
                    a = v[:, h, :, 0, yy].reshape(4, 8, v.shape[-1])
                    b = v[:, h, :, 1, yy].reshape(4, 8, v.shape[-1])
                    for cc, tile in enumerate(zip_rows(a, b)):
                        part[r, cc, h * 2 + yy, 4 * m : 4 * m + 4, :, cols] = tile
        at = pl.ds(4 * m, 4)
        ex.send(2 * r + m, part.at[r, 1 - c, :, at], pair.at[r, :, at], other)

    def ring1(r, m):
        k = 6 * (2 * r + m)
        at, lo, hi = pl.ds(4 * m, 4), pl.ds(4 * m, 2), pl.ds(4 * m + 2, 2)
        ex.take(2 * r + m, pair.at[r, :, at], other)
        part[r, c, :, at] = part[r, c, :, at] + pair[r, :, at]
        rs.send(k + 0, part.at[r, c, far, lo], ring_o.at[r, 0, m], up)
        rs.send(k + 1, part.at[r, c, far, hi], ring_o.at[r, 1, m], down)
        rs.send(k + 2, part.at[r, c, above, hi], ring_n.at[r, 0, hi], up)
        rs.send(k + 3, part.at[r, c, below, lo], ring_n.at[r, 1, lo], down)

    def ring2(r, m):
        k = 6 * (2 * r + m)
        lo, hi = pl.ds(4 * m, 2), pl.ds(4 * m + 2, 2)
        rs.take(k + 0, ring_o.at[r, 0, m], up)
        part[r, c, above, lo] = part[r, c, above, lo] + ring_o[r, 0, m]
        rs.send(k + 4, part.at[r, c, above, lo], ring_n.at[r, 0, lo], up)
        rs.take(k + 1, ring_o.at[r, 1, m], up)
        part[r, c, below, hi] = part[r, c, below, hi] + ring_o[r, 1, m]
        rs.send(k + 5, part.at[r, c, below, hi], ring_n.at[r, 1, hi], down)

    def shift(a, b):
        return jnp.where(y < 2, b, a), jnp.where(y < 2, a, b)

    def finish(r, m):
        k = 6 * (2 * r + m)
        at, lo, hi = pl.ds(4 * m, 4), pl.ds(4 * m, 2), pl.ds(4 * m + 2, 2)
        rs.take(k + 2, ring_n.at[r, 0, hi], up)
        rs.take(k + 3, ring_n.at[r, 1, lo], up)
        rs.take(k + 4, ring_n.at[r, 0, lo], up)
        rs.take(k + 5, ring_n.at[r, 1, hi], up)
        qsend[r, at] = (part[r, c, y, at] + ring_n[r, 0, at] + ring_n[r, 1, at]).astype(BF16)
        for i in (2 * m, 2 * m + 1):
            for s, (a, b) in enumerate(SLOTS[i]):
                k = 4 * i + s
                if k == 0:
                    qrecv[r, 0] = qsend[r, 0]
                    continue
                dz, dx = shift(a, b)
                target = (m4(z + dz) * 4 + m4(x + dx), n)
                aa.send(16 * r + k, qsend.at[r, k // 2], qrecv.at[r, k], target)

    def receive(r):
        for i in range(4):
            for s, (a, b) in enumerate(SLOTS[i]):
                k = 4 * i + s
                if k:
                    aa.take(16 * r + k, qrecv.at[r, k], other)
                dz, dx = shift(a, b)
                tile = qrecv[r, k].astype(F32)
                if s % 2:
                    tile = pltpu.roll(tile, 4, 0)
                qx[m4(z - dz) * 4 + m4(x - dx)] = tile
        cos, sin = turns[r]

        def turn(v):
            return (v * cos + pltpu.roll(v, 64, v.ndim - 1) * sin).astype(BF16)

        low = lax.broadcasted_iota(jnp.int32, (1, 8, 128), 1) < 4
        for p in range(2):
            a = turn(qx[:, :, p * 256 : p * 256 + 128]).astype(F32)
            b = turn(qx[:, :, p * 256 + 128 : p * 256 + 256]).astype(F32)
            tile = jnp.where(low, a, pltpu.roll(b, 4, 1))
            for h in range(4):
                gi = h % 2
                qs[h // 2, gi * 64 + p * 32 : gi * 64 + p * 32 + 32,
                   gi * 128 : gi * 128 + 128] = (
                    tile[4 * h : 4 * h + 4].reshape(32, 128).astype(BF16)
                )
        for h in range(4):
            cols = slice(h * 128, h * 128 + 128)
            key = jnp.concatenate([qx[2 * h, :, 512:576], qx[2 * h + 1, :, 512:576]], -1)
            val = jnp.concatenate([qx[2 * h + 8, :, 512:576], qx[2 * h + 9, :, 512:576]], -1)
            key = turn(key)
            kf[0:8, cols] = key
            vf[0:8, cols] = val.astype(BF16)
            kvout[r, 0, :, cols] = key.astype(F32)
            kvout[r, 1, :, cols] = val

    factor = 1.0 / jnp.sqrt(F32(HD))

    def attend(r, gp):
        lane = lax.broadcasted_iota(jnp.int32, (128, 128), 1)
        step = lax.rem(lax.broadcasted_iota(jnp.int32, (128, 128), 0), 4)
        place = lax.broadcasted_iota(jnp.int32, (128, CHUNK), 1)
        q = qs[gp]
        cols = pl.ds(gp * 256, 256)
        length = len_ref[r]
        fs = lax.dot_general(q, kf[:, cols], NT, preferred_element_type=F32) * factor
        fs = jnp.where(lane <= step, fs, -jnp.inf)

        def score(j, top):
            at = pl.ds(pl.multiple_of(j * CHUNK, CHUNK), CHUNK)
            s = lax.dot_general(q, kb[r, at, cols], NT, preferred_element_type=F32) * factor
            s = jnp.where(place < length - j * CHUNK, s, -jnp.inf)
            sc[:, at] = s
            for u in range(CHUNK // 128):
                top = jnp.maximum(top, s[:, u * 128 : u * 128 + 128])
            return top

        top = lax.fori_loop(0, 4096 // CHUNK, score, fs)
        top = jnp.max(top, axis=-1, keepdims=True)
        fe = jnp.exp(fs - top)

        def expo(j, acc):
            at = pl.ds(pl.multiple_of(j * CHUNK, CHUNK), CHUNK)
            e = jnp.exp(sc[:, at] - top)
            sc[:, at] = e
            for u in range(CHUNK // 128):
                acc = acc + e[:, u * 128 : u * 128 + 128]
            return acc

        acc = lax.fori_loop(0, 4096 // CHUNK, expo, fe)
        scale = 1.0 / jnp.sum(acc, axis=-1, keepdims=True)

        def value(j, out):
            at = pl.ds(pl.multiple_of(j * CHUNK, CHUNK), CHUNK)
            p = (sc[:, at] * scale).astype(BF16)
            return out + jnp.dot(p, vb[r, at, cols], preferred_element_type=F32)

        out = jnp.dot((fe * scale).astype(BF16), vf[:, cols], preferred_element_type=F32)
        out = lax.fori_loop(0, 4096 // CHUNK, value, out)
        for gi in range(2):
            v = out[gi * 64 : gi * 64 + 64, gi * 128 : gi * 128 + 128].reshape(2, 4, 8, 128)
            h = 2 * gp + gi
            att[r, 4 * h : 4 * h + 4, :, 0:128] = v[0].astype(BF16)
            att[r, 4 * h : 4 * h + 4, :, 128:256] = v[1].astype(BF16)

    ao, gn = Copies(ao_s, ao_r), Copies(gn_s, gn_r)
    na, nb, nf = above * 2 + c, below * 2 + c, far * 2 + c
    lo8, hi8 = pl.ds(0, 8), pl.ds(8, 8)

    def spread_heads(r):
        for i in range(1, 16):
            peer = lax.rem(w + i, 16)
            ao.send(15 * r + i - 1, att.at[r, peer], g.at[r, n, w], (peer, n))
        g[r, n, w] = att[r, w]

    def narrow1(r):
        k = 8 * r
        for i in range(1, 16):
            ao.take(15 * r + i - 1, g.at[r, n, lax.rem(w - i + 16, 16)], other)
        gn.send(k + 0, g.at[r, n], g.at[r, n], up)
        gn.send(k + 1, g.at[r, n], g.at[r, n], down)
        gn.send(k + 2, g.at[r, n], g.at[r, n], other)

    def narrow2(r):
        k = 8 * r
        gn.take(k + 0, g.at[r, nb], up)
        gn.send(k + 3, g.at[r, nb, lo8], g.at[r, nb, lo8], up)
        gn.send(k + 4, g.at[r, nb], g.at[r, nb], other)
        gn.take(k + 1, g.at[r, na], up)
        gn.send(k + 5, g.at[r, na, hi8], g.at[r, na, hi8], down)
        gn.send(k + 6, g.at[r, na], g.at[r, na], other)

    def narrow3(r):
        k = 8 * r
        gn.take(k + 3, g.at[r, nf, lo8], up)
        gn.take(k + 5, g.at[r, nf, hi8], up)
        gn.send(k + 7, g.at[r, nf], g.at[r, nf], other)
        gn.take(k + 2, g.at[r, y * 2 + 1 - c], up)
        gn.take(k + 4, g.at[r, below * 2 + 1 - c], up)
        gn.take(k + 6, g.at[r, above * 2 + 1 - c], up)
        gn.take(k + 7, g.at[r, far * 2 + 1 - c], up)

        def regroup(i, carry):
            v = g[r, :, i].astype(F32).reshape(4, 2, 8, 256)
            for hl, tile in enumerate(zip_rows(v[:, 0], v[:, 1])):
                tile = tile.reshape(32, 256).astype(BF16)
                for p in range(2):
                    at = p * 256 + hl * 128
                    gm[i, :, at : at + 128] = tile[:, p * 128 : p * 128 + 128]
            return carry

        lax.fori_loop(0, 16, regroup, 0)

    st, st2 = Copies(st_s, st_r), Copies(st2_s, st2_r)
    halves = (
        (0, lambda a, b: m4(z + b) * 4 + m4(x + a), along_x, along_z),
        (1, lambda a, b: m4(z + a) * 4 + m4(x + b), along_z, along_x),
    )
    top16, bot16 = pl.ds(0, 16), pl.ds(16, 16)
    two = (pl.ds(0, 2), pl.ds(2, 2))

    def product(h, index, a):
        lhs = jnp.concatenate([gm[index(a, b)] for b in OFFSETS], axis=0)
        cols = slice(h * 1024, h * 1024 + 1024)
        v = jnp.dot(lhs, wo[:, cols], preferred_element_type=F32)
        return v.reshape(4, 32, 1024)

    def products(r):
        for h, index, to1, to2 in halves:
            k = 24 * r + 12 * h
            v = product(h, index, 2)
            so[r, h, 0] = v[:, 0:16].astype(BF16)
            so[r, h, 1] = v[:, 16:32].astype(BF16)
            for u, q in enumerate(two):
                st.send(k + u, so.at[r, h, 0, q], ro.at[r, h, 0, q], to1(1))
                st.send(k + 2 + u, so.at[r, h, 1, q], ro.at[r, h, 1, q], to1(-1))
        for h, index, to1, to2 in halves:
            k = 24 * r + 12 * h
            v = product(h, index, 1)
            sn[r, h, 0, :, 16:32] = v[:, 16:32].astype(BF16)
            kp[r, h, 0] = v[:, 0:16]
            for u, q in enumerate(two):
                st.send(
                    k + 4 + u, sn.at[r, h, 0, q, bot16], rn.at[r, h, 0, q, bot16], to1(1)
                )
            v = product(h, index, -1)
            sn[r, h, 1, :, 0:16] = v[:, 0:16].astype(BF16)
            kp[r, h, 1] = v[:, 16:32]
            for u, q in enumerate(two):
                st.send(
                    k + 6 + u, sn.at[r, h, 1, q, top16], rn.at[r, h, 1, q, top16], to1(-1)
                )
        for h, index, to1, to2 in halves:
            km[r, h] = product(h, index, 0)

    def relay(r):
        for u, q in enumerate(two):
            qq = slice(2 * u, 2 * u + 2)
            for h, index, to1, to2 in halves:
                k = 24 * r + 12 * h
                st.take(k + u, ro.at[r, h, 0, q], to1(1))
                sn[r, h, 0, qq, 0:16] = (
                    kp[r, h, 0, qq] + ro[r, h, 0, qq].astype(F32)
                ).astype(BF16)
                st.send(k + 8 + u, sn.at[r, h, 0, q, top16], rn.at[r, h, 0, q, top16], to1(1))
                st.take(k + 2 + u, ro.at[r, h, 1, q], to1(1))
                sn[r, h, 1, qq, 16:32] = (
                    kp[r, h, 1, qq] + ro[r, h, 1, qq].astype(F32)
                ).astype(BF16)
                st.send(k + 10 + u, sn.at[r, h, 1, q, bot16], rn.at[r, h, 1, q, bot16], to1(-1))

    def second(r):
        for u, q in enumerate(two):
            for h, index, to1, to2 in halves:
                k, k2 = 24 * r + 12 * h, 12 * r + 6 * h
                st.take(k + 4 + u, rn.at[r, h, 0, q, bot16], to1(1))
                st.take(k + 6 + u, rn.at[r, h, 1, q, top16], to1(1))
                st.take(k + 8 + u, rn.at[r, h, 0, q, top16], to1(1))
                st.take(k + 10 + u, rn.at[r, h, 1, q, bot16], to1(1))
                for i in (2 * u, 2 * u + 1):
                    v = km[r, h, i] + rn[r, h, 0, i].astype(F32) + rn[r, h, 1, i].astype(F32)
                    if i == 0:
                        so2[r, h] = v.reshape(2, 16, 1024).astype(BF16)
                        st2.send(k2 + 0, so2.at[r, h, 0], ro2.at[r, h, 0], to2(1))
                        st2.send(k2 + 1, so2.at[r, h, 1], ro2.at[r, h, 1], to2(-1))
                        continue
                    km[r, h, i] = v
                    if i == 1:
                        sn2[r, h, 0, 16:32] = v[16:32].astype(BF16)
                        st2.send(k2 + 2, sn2.at[r, h, 0, bot16], rn2.at[r, h, 0, bot16], to2(1))
                    elif i == 2:
                        sn2[r, h, 1, 0:16] = v[0:16].astype(BF16)
                        st2.send(k2 + 3, sn2.at[r, h, 1, top16], rn2.at[r, h, 1, top16], to2(-1))
        for h, index, to1, to2 in halves:
            k2 = 12 * r + 6 * h
            st2.take(k2 + 0, ro2.at[r, h, 0], to1(1))
            sn2[r, h, 0, 0:16] = (km[r, h, 1, 0:16] + ro2[r, h, 0].astype(F32)).astype(BF16)
            st2.send(k2 + 4, sn2.at[r, h, 0, top16], rn2.at[r, h, 0, top16], to2(1))
            st2.take(k2 + 1, ro2.at[r, h, 1], to1(1))
            sn2[r, h, 1, 16:32] = (km[r, h, 2, 16:32] + ro2[r, h, 1].astype(F32)).astype(BF16)
            st2.send(k2 + 5, sn2.at[r, h, 1, bot16], rn2.at[r, h, 1, bot16], to2(-1))

    def total_rows(r):
        for h, index, to1, to2 in halves:
            k2 = 12 * r + 6 * h
            st2.take(k2 + 2, rn2.at[r, h, 0, bot16], to1(1))
            st2.take(k2 + 3, rn2.at[r, h, 1, top16], to1(1))
            st2.take(k2 + 4, rn2.at[r, h, 0, top16], to1(1))
            st2.take(k2 + 5, rn2.at[r, h, 1, bot16], to1(1))
            for j in range(8):
                sub = slice(j * 128, j * 128 + 128)
                res[h * 8 + j] = (
                    km[r, h, 3, :, sub]
                    + rn2[r, h, 0, :, sub].astype(F32)
                    + rn2[r, h, 1, :, sub].astype(F32)
                )
        for j in range(16):
            for t in range(4):
                rows16[j, t, pl.ds(r, 8, stride=2), :] = res[j, pl.ds(t, 8, stride=4), :]

    gather(0, 0, 1, 2, 3, 4, 5)
    loads[2].wait()
    loads[3].wait()
    multiply(0, 0)
    gather(1, 0, 1)
    gather(0, 6)
    ring1(0, 0)
    gather(0, 7)
    multiply(0, 1)
    gather(1, 2, 3)
    ring2(0, 0)
    ring1(0, 1)
    gather(1, 4, 5)
    finish(0, 0)
    ring2(0, 1)
    multiply(1, 0)
    gather(1, 6)
    finish(0, 1)
    ring1(1, 0)
    gather(1, 7)
    multiply(1, 1)
    ring2(1, 0)
    receive(0)
    ring1(1, 1)
    loads[5].wait()
    loads[6].wait()
    attend(0, 0)
    finish(1, 0)
    ring2(1, 1)
    attend(0, 1)
    spread_heads(0)
    finish(1, 1)
    narrow1(0)
    receive(1)
    attend(1, 0)
    narrow2(0)
    attend(1, 1)
    spread_heads(1)
    loads[4].wait()
    narrow3(0)
    products(0)
    narrow1(1)
    relay(0)
    narrow2(1)
    narrow3(1)
    products(1)
    second(0)
    relay(1)
    total_rows(0)
    second(1)
    total_rows(1)
    for j in range(16):
        for t in range(4):
            out_ref[t, :, j * 128 : j * 128 + 128] = rows16[j, t].astype(BF16)
    nk[...] = zip_rows(kvout[0, 0], kvout[1, 0])[0].astype(BF16)
    nv[...] = zip_rows(kvout[0, 1], kvout[1, 1])[0].astype(BF16)
    for group in (sqc, ag, ex, rs, aa, ao, gn, st, st2):
        group.drain()


def local(inputs, norm_gain, w_query, w_keyval, w_out, key_cache, value_cache, lengths, positions):
    dma = pltpu.SemaphoreType.DMA
    vm = pl.BlockSpec(memory_space=pltpu.VMEM)
    sm = pl.BlockSpec(memory_space=pltpu.SMEM)
    hbm = pl.BlockSpec(memory_space=pl.ANY)

    def b16(*shape):
        return pltpu.VMEM(shape, BF16)

    def f32(*shape):
        return pltpu.VMEM(shape, F32)

    attended, nk, nv = pl.pallas_call(
        layer_kernel,
        out_shape=(
            jax.ShapeDtypeStruct((4, 16, 2048), BF16),
            jax.ShapeDtypeStruct((8, 512), BF16),
            jax.ShapeDtypeStruct((8, 512), BF16),
        ),
        in_specs=[sm, sm] + [hbm] * 7,
        out_specs=(vm, vm, vm),
        scratch_shapes=[
            b16(4, 16, 2048), b16(2048), b16(2048, 512), b16(64, 2048), b16(512, 2048),
            b16(2, 4096, 512), b16(2, 4096, 512),
            f32(16, 64, 128), f32(8, 128), f32(7, 8, 128), b16(2, 4, 2, 4, 16, 2048),
            f32(2, 2, 4, 8, 8, 576), f32(2, 4, 8, 8, 576), f32(2, 2, 2, 2, 8, 576),
            f32(2, 2, 8, 8, 576), b16(2, 8, 8, 576), b16(2, 16, 8, 576), f32(16, 8, 576),
            b16(2, 128, 256), b16(128, 512), b16(128, 512), f32(2, 2, 8, 512), f32(128, 4096),
            b16(2, 16, 8, 256), b16(2, 8, 16, 8, 256), b16(16, 32, 512),
            b16(2, 2, 2, 4, 16, 1024), b16(2, 2, 2, 4, 32, 1024),
            b16(2, 2, 2, 4, 16, 1024), b16(2, 2, 2, 4, 32, 1024),
            f32(2, 2, 2, 4, 16, 1024), f32(2, 2, 4, 32, 1024),
            b16(2, 2, 2, 16, 1024), b16(2, 2, 2, 32, 1024),
            b16(2, 2, 2, 16, 1024), b16(2, 2, 2, 32, 1024),
            f32(16, 32, 128), f32(16, 4, 16, 128),
            dma((7,)), dma((7,)), dma((7,)), dma((80,)), dma((80,)), dma((4,)), dma((4,)),
            dma((24,)), dma((24,)), dma((32,)), dma((32,)), dma((30,)), dma((30,)),
            dma((16,)), dma((16,)), dma((48,)), dma((48,)), dma((24,)), dma((24,)),
        ],
        compiler_params=pltpu.CompilerParams(
            collective_id=0, has_side_effects=True, vmem_limit_bytes=60 << 20
        ),
        name="layer",
    )(
        lengths, positions, inputs, norm_gain, w_query, w_keyval.T, w_out,
        key_cache, value_cache,
    )

    def by_step(a):
        return a.reshape(2, STEPS, KVH * HD).transpose(1, 0, 2)

    return attended, by_step(nk), by_step(nv)


def solution(mesh):
    return jax.shard_map(
        local,
        mesh=mesh,
        in_specs=(
            P(None, "wide", "narrow"),
            P("narrow"),
            P("narrow", "wide"),
            P("narrow", "wide"),
            P("wide", "narrow"),
            P(("wide", "narrow"), None, None),
            P(("wide", "narrow"), None, None),
            P(("wide", "narrow")),
            P(("wide", "narrow")),
        ),
        out_specs=(
            P(None, "wide", "narrow"),
            P(None, ("wide", "narrow"), None),
            P(None, ("wide", "narrow"), None),
        ),
        check_vma=False,
    )
```

time: 114 us -> 109 us (0.956); the launches traced: 112 us -> 109 us
  local copies, waits for them, and re-layouts: 5.67 us -> 3.7 us
  other arithmetic: 1.52 us -> 0 us
    reshape x1 -> x0, local copies, waits for them, and re-layouts: 1.29 us -> none  [local(): norm_gain.reshape(1, 2048)]
    reshape x4 -> x2, local copies, waits for them, and re-layouts: 2.63 us -> 1.41 us  [by_step(): return a.reshape(2, STEPS, KVH * HD).transpose(1, 0, 2)]
where the time goes in v3:
time: 109 us
  Pallas kernels  104 us (95%)
  local copies, waits for them, and re-layouts  3.7 us (3%)
    pallas_call x1, Pallas kernels, local(): pl.pallas_call(layer_kernel, out_shape=(jax.ShapeDtypeStruct((4, 16, 2048...  104 us

profile of v3, /device:TPU:0, one launch (start us, length us, event | category | flops | bytes accessed | tf_op | source)
XLA Modules:
  0.0 108.6 jit_solution(7904642524629306827)
XLA Ops:
  0.6 104.3 %layer.1 = (bf16[4,16,2048]{2,1,0:T(8,128)(2,1)}, bf16[8,512]{1,0:T(8,128)(2,1)}, bf16[8,512]{1,0:T(8,128)(2,1)}) custom-call(s32[2]{0:T(128)} %len_ref.1, s32[2]{0:T(128)} %pos_ref.1, bf16[4,16,2048]{2,1,0:T(8,128)(2,1)} %x_hbm.1, bf16[2048]{0:T(1024)(128)(2,1)} %gain_hbm.1, bf16[2048,512]{1,0:T(8,128)(2,1)} %wq_hbm.1, bf16[64,2048]{1,0:T(8,128)(2,1)} %bitcast.5, ...), custom_call_target="tpu_custom_call" | custom-call | tf_op jit(solution)/shard_map/layer/pallas_call | solution.py:620
  104.9 0.7 reshape.12
  105.6 0.7 reshape.13
  106.3 0.6 copy_bitcast_fusion
  106.9 1.7 %copy.17 = bf16[4,16,2048]{2,1,0:T(8,128)(2,1)} copy(bf16[4,16,2048]{2,1,0:T(8,128)(2,1)} %get-tuple-element.14) | data formatting | bytes 524288

commit v4 on v3

--- a/solution.py
+++ b/solution.py
@@ -142,8 +142,8 @@
 
 def layer_kernel(
     len_ref, pos_ref, x_hbm, gain_hbm, wq_hbm, wkv_hbm, wo_hbm, k_hbm, v_hbm,
-    out_ref, nk, nv,
-    xv, gain, wq, wkv, wo, kb, vb,
+    out_hbm, nk_hbm, nv_hbm,
+    out_ref, nk, nv, xv, gain, wq, wkv, wo, kb, vb,
     xs, sq, sqr, buf, part, pair, ring_o, ring_n, qsend, qrecv, qx,
     qs, kf, vf, kvout, sc, att, g, gm,
     so, sn, ro, rn, kp, km, so2, sn2, ro2, rn2, res, rows16,
@@ -162,6 +162,7 @@
 
     other = (w, y * 2 + (1 - c))
     up, down = (w, m4(y + 1) * 2 + c), (w, m4(y - 1) * 2 + c)
+    up2, down2 = (w, m4(y + 1) * 2 + 1 - c), (w, m4(y - 1) * 2 + 1 - c)
     far, above, below = m4(y + 2), m4(y + 1), m4(y - 1)
 
     barrier = pltpu.get_barrier_semaphore()
@@ -338,8 +339,8 @@
             key = turn(key)
             kf[0:8, cols] = key
             vf[0:8, cols] = val.astype(BF16)
-            kvout[r, 0, :, cols] = key.astype(F32)
-            kvout[r, 1, :, cols] = val
+            kvout[0, h, pl.ds(r, 4, stride=2), :] = key.astype(F32)[0:4]
+            kvout[1, h, pl.ds(r, 4, stride=2), :] = val[0:4]
 
     factor = 1.0 / jnp.sqrt(F32(HD))
 
@@ -401,7 +402,7 @@
         g[r, n, w] = att[r, w]
 
     def narrow1(r):
-        k = 8 * r
+        k = 10 * r
         for i in range(1, 16):
             ao.take(15 * r + i - 1, g.at[r, n, lax.rem(w - i + 16, 16)], other)
         gn.send(k + 0, g.at[r, n], g.at[r, n], up)
@@ -409,23 +410,25 @@
         gn.send(k + 2, g.at[r, n], g.at[r, n], other)
 
     def narrow2(r):
-        k = 8 * r
+        k = 10 * r
         gn.take(k + 0, g.at[r, nb], up)
         gn.send(k + 3, g.at[r, nb, lo8], g.at[r, nb, lo8], up)
+        gn.send(k + 8, g.at[r, nb, lo8], g.at[r, nb, lo8], up2)
         gn.send(k + 4, g.at[r, nb], g.at[r, nb], other)
         gn.take(k + 1, g.at[r, na], up)
         gn.send(k + 5, g.at[r, na, hi8], g.at[r, na, hi8], down)
+        gn.send(k + 9, g.at[r, na, hi8], g.at[r, na, hi8], down2)
         gn.send(k + 6, g.at[r, na], g.at[r, na], other)
 
     def narrow3(r):
-        k = 8 * r
+        k = 10 * r
         gn.take(k + 3, g.at[r, nf, lo8], up)
         gn.take(k + 5, g.at[r, nf, hi8], up)
-        gn.send(k + 7, g.at[r, nf], g.at[r, nf], other)
         gn.take(k + 2, g.at[r, y * 2 + 1 - c], up)
         gn.take(k + 4, g.at[r, below * 2 + 1 - c], up)
         gn.take(k + 6, g.at[r, above * 2 + 1 - c], up)
-        gn.take(k + 7, g.at[r, far * 2 + 1 - c], up)
+        gn.take(k + 8, g.at[r, far * 2 + 1 - c, lo8], up)
+        gn.take(k + 9, g.at[r, far * 2 + 1 - c, hi8], up)
 
         def regroup(i, carry):
             v = g[r, :, i].astype(F32).reshape(4, 2, 8, 256)
@@ -518,6 +521,8 @@
                     elif i == 2:
                         sn2[r, h, 1, 0:16] = v[0:16].astype(BF16)
                         st2.send(k2 + 3, sn2.at[r, h, 1, top16], rn2.at[r, h, 1, top16], to2(-1))
+
+    def relay2(r):
         for h, index, to1, to2 in halves:
             k2 = 12 * r + 6 * h
             st2.take(k2 + 0, ro2.at[r, h, 0], to1(1))
@@ -541,48 +546,76 @@
                     + rn2[r, h, 0, :, sub].astype(F32)
                     + rn2[r, h, 1, :, sub].astype(F32)
                 )
-        for j in range(16):
-            for t in range(4):
-                rows16[j, t, pl.ds(r, 8, stride=2), :] = res[j, pl.ds(t, 8, stride=4), :]
-
-    gather(0, 0, 1, 2, 3, 4, 5)
+            for j in range(h * 8, h * 8 + 8):
+                for t in range(4):
+                    rows16[j, t, pl.ds(r, 8, stride=2), :] = res[j, pl.ds(t, 8, stride=4), :]
+            if r == 1:
+                for j in range(h * 8, h * 8 + 8):
+                    for t in range(4):
+                        out_ref[t, :, j * 128 : j * 128 + 128] = rows16[j, t].astype(BF16)
+                cols = pl.ds(h * 1024, 1024)
+                store = pltpu.make_async_copy(
+                    out_ref.at[:, :, cols], out_hbm.at[:, :, cols], ld.at[9 + h]
+                )
+                store.start()
+                stores.append(store)
+
+    def new_rows():
+        for t in range(4):
+            for h in range(4):
+                cols = slice(h * 128, h * 128 + 128)
+                nk[t, :, cols] = kvout[0, h, 2 * t : 2 * t + 2].astype(BF16)
+                nv[t, :, cols] = kvout[1, h, 2 * t : 2 * t + 2].astype(BF16)
+        for i, (source, target) in enumerate(((nk, nk_hbm), (nv, nv_hbm))):
+            store = pltpu.make_async_copy(source, target, ld.at[7 + i])
+            store.start()
+            stores.append(store)
+
+    stores = []
+
+    gather(0, 0, 1, 2)
+    gather(1, 0, 1)
+    gather(0, 3, 4)
+    gather(1, 2)
+    gather(0, 5)
     loads[2].wait()
     loads[3].wait()
     multiply(0, 0)
-    gather(1, 0, 1)
+    gather(1, 3)
     gather(0, 6)
+    gather(1, 4)
     ring1(0, 0)
     gather(0, 7)
     multiply(0, 1)
-    gather(1, 2, 3)
+    gather(1, 5)
     ring2(0, 0)
-    ring1(0, 1)
-    gather(1, 4, 5)
-    finish(0, 0)
-    ring2(0, 1)
     multiply(1, 0)
     gather(1, 6)
-    finish(0, 1)
-    ring1(1, 0)
+    finish(0, 0)
+    ring1(0, 1)
     gather(1, 7)
     multiply(1, 1)
+    ring1(1, 0)
+    ring2(0, 1)
     ring2(1, 0)
+    finish(0, 1)
+    ring1(1, 1)
+    finish(1, 0)
+    ring2(1, 1)
     receive(0)
-    ring1(1, 1)
     loads[5].wait()
     loads[6].wait()
     attend(0, 0)
-    finish(1, 0)
-    ring2(1, 1)
+    finish(1, 1)
     attend(0, 1)
     spread_heads(0)
-    finish(1, 1)
-    narrow1(0)
     receive(1)
     attend(1, 0)
-    narrow2(0)
+    narrow1(0)
     attend(1, 1)
     spread_heads(1)
+    new_rows()
+    narrow2(0)
     loads[4].wait()
     narrow3(0)
     products(0)
@@ -590,26 +623,24 @@
     relay(0)
     narrow2(1)
     narrow3(1)
+    second(0)
     products(1)
-    second(0)
     relay(1)
+    relay2(0)
+    second(1)
     total_rows(0)
-    second(1)
+    relay2(1)
     total_rows(1)
-    for j in range(16):
-        for t in range(4):
-            out_ref[t, :, j * 128 : j * 128 + 128] = rows16[j, t].astype(BF16)
-    nk[...] = zip_rows(kvout[0, 0], kvout[1, 0])[0].astype(BF16)
-    nv[...] = zip_rows(kvout[0, 1], kvout[1, 1])[0].astype(BF16)
+    for store in stores:
+        store.wait()
     for group in (sqc, ag, ex, rs, aa, ao, gn, st, st2):
         group.drain()
 
 
 def local(inputs, norm_gain, w_query, w_keyval, w_out, key_cache, value_cache, lengths, positions):
     dma = pltpu.SemaphoreType.DMA
-    vm = pl.BlockSpec(memory_space=pltpu.VMEM)
     sm = pl.BlockSpec(memory_space=pltpu.SMEM)
-    hbm = pl.BlockSpec(memory_space=pl.ANY)
+    hbm = pl.BlockSpec(memory_space=pltpu.HBM)
 
     def b16(*shape):
         return pltpu.VMEM(shape, BF16)
@@ -617,22 +648,23 @@
     def f32(*shape):
         return pltpu.VMEM(shape, F32)
 
-    attended, nk, nv = pl.pallas_call(
+    return pl.pallas_call(
         layer_kernel,
         out_shape=(
             jax.ShapeDtypeStruct((4, 16, 2048), BF16),
-            jax.ShapeDtypeStruct((8, 512), BF16),
-            jax.ShapeDtypeStruct((8, 512), BF16),
+            jax.ShapeDtypeStruct((4, 2, 512), BF16),
+            jax.ShapeDtypeStruct((4, 2, 512), BF16),
         ),
         in_specs=[sm, sm] + [hbm] * 7,
-        out_specs=(vm, vm, vm),
+        out_specs=(hbm, hbm, hbm),
         scratch_shapes=[
+            b16(4, 16, 2048), b16(4, 2, 512), b16(4, 2, 512),
             b16(4, 16, 2048), b16(2048), b16(2048, 512), b16(64, 2048), b16(512, 2048),
             b16(2, 4096, 512), b16(2, 4096, 512),
             f32(16, 64, 128), f32(8, 128), f32(7, 8, 128), b16(2, 4, 2, 4, 16, 2048),
             f32(2, 2, 4, 8, 8, 576), f32(2, 4, 8, 8, 576), f32(2, 2, 2, 2, 8, 576),
             f32(2, 2, 8, 8, 576), b16(2, 8, 8, 576), b16(2, 16, 8, 576), f32(16, 8, 576),
-            b16(2, 128, 256), b16(128, 512), b16(128, 512), f32(2, 2, 8, 512), f32(128, 4096),
+            b16(2, 128, 256), b16(128, 512), b16(128, 512), f32(2, 4, 8, 128), f32(128, 4096),
             b16(2, 16, 8, 256), b16(2, 8, 16, 8, 256), b16(16, 32, 512),
             b16(2, 2, 2, 4, 16, 1024), b16(2, 2, 2, 4, 32, 1024),
             b16(2, 2, 2, 4, 16, 1024), b16(2, 2, 2, 4, 32, 1024),
@@ -640,9 +672,9 @@
             b16(2, 2, 2, 16, 1024), b16(2, 2, 2, 32, 1024),
             b16(2, 2, 2, 16, 1024), b16(2, 2, 2, 32, 1024),
             f32(16, 32, 128), f32(16, 4, 16, 128),
-            dma((7,)), dma((7,)), dma((7,)), dma((80,)), dma((80,)), dma((4,)), dma((4,)),
+            dma((11,)), dma((7,)), dma((7,)), dma((80,)), dma((80,)), dma((4,)), dma((4,)),
             dma((24,)), dma((24,)), dma((32,)), dma((32,)), dma((30,)), dma((30,)),
-            dma((16,)), dma((16,)), dma((48,)), dma((48,)), dma((24,)), dma((24,)),
+            dma((20,)), dma((20,)), dma((48,)), dma((48,)), dma((24,)), dma((24,)),
         ],
         compiler_params=pltpu.CompilerParams(
             collective_id=0, has_side_effects=True, vmem_limit_bytes=60 << 20
@@ -652,11 +684,6 @@
         lengths, positions, inputs, norm_gain, w_query, w_keyval.T, w_out,
         key_cache, value_cache,
     )
-
-    def by_step(a):
-        return a.reshape(2, STEPS, KVH * HD).transpose(1, 0, 2)
-
-    return attended, by_step(nk), by_step(nv)
 
 
 def solution(mesh):

time: 109 us -> 110 us (level)
    unnamed x1 -> x3, local copies, waits for them, and re-layouts: 1.67 us -> 4.27 us
    reshape x2 -> x0, local copies, waits for them, and re-layouts: 1.41 us -> none  [by_step(): return a.reshape(2, STEPS, KVH * HD).transpose(1, 0, 2)]
where the time goes in v4:
time: 110 us
  Pallas kernels  105 us (95%)
  local copies, waits for them, and re-layouts  4.27 us (4%)
    pallas_call x1, Pallas kernels, local(): pl.pallas_call(layer_kernel, out_shape=(jax.ShapeDtypeStruct((4, 16, 2048...  105 us
    unnamed x3, local copies, waits for them, and re-layouts  4.27 us

profile of v4, /device:TPU:0, one launch (start us, length us, event | category | flops | bytes accessed | tf_op | source)
XLA Modules:
  0.0 109.8 jit_solution(17163962456979285053)
XLA Ops:
  0.6 104.9 %layer.1 = (bf16[4,16,2048]{2,1,0:T(8,128)(2,1)}, bf16[4,2,512]{2,1,0:T(2,128)(2,1)}, bf16[4,2,512]{2,1,0:T(2,128)(2,1)}) custom-call(s32[2]{0:T(128)} %len_ref.1, s32[2]{0:T(128)} %pos_ref.1, bf16[4,16,2048]{2,1,0:T(8,128)(2,1)} %x_hbm.1, bf16[2048]{0:T(1024)(128)(2,1)} %gain_hbm.1, bf16[2048,512]{1,0:T(8,128)(2,1)} %wq_hbm.1, bf16[64,2048]{1,0:T(8,128)(2,1)} %bitcast.1, ...), custom_call_target="tpu_custom_call" | custom-call | tf_op jit(solution)/shard_map/layer/pallas_call | solution.py:651
  105.5 1.7 %copy.15 = bf16[4,16,2048]{2,1,0:T(8,128)(2,1)} copy(bf16[4,16,2048]{2,1,0:T(8,128)(2,1)} %get-tuple-element.6) | data formatting | bytes 524288
  107.2 1.3 %copy.16 = bf16[4,2,512]{2,1,0:T(2,128)(2,1)} copy(bf16[4,2,512]{2,1,0:T(2,128)(2,1)} %get-tuple-element.7) | data formatting | bytes 16384
  108.5 1.3 %copy.17 = bf16[4,2,512]{2,1,0:T(2,128)(2,1)} copy(bf16[4,2,512]{2,1,0:T(2,128)(2,1)} %get-tuple-element.8) | data formatting | bytes 16384

commit v5 on v4

--- a/solution.py
+++ b/solution.py
@@ -50,12 +50,12 @@
         self.ssem, self.rsem, self.sent = ssem, rsem, []
 
     def send(self, k, src, dst, target):
-        c = rcopy(src, dst, self.ssem.at[k], self.rsem.at[k], target)
+        c = rcopy(src, dst, self.ssem, self.rsem.at[k], target)
         c.start()
         self.sent.append(c)
 
     def take(self, k, dst, target):
-        rcopy(dst, dst, self.ssem.at[k], self.rsem.at[k], target).wait_recv()
+        rcopy(dst, dst, self.ssem, self.rsem.at[k], target).wait_recv()
 
     def drain(self):
         for c in self.sent:
@@ -79,18 +79,17 @@
         cp.take(k0 + k, at(a, b, cols), to1(1))
 
     def spread(j, a):
-        send2(4 + 4 * j, a, 0, full, 1)
-        send2(5 + 4 * j, a, 0, full, -1)
+        send2(3 + 3 * j, a, 0, full, 1)
+        send2(4 + 3 * j, a, 0, full, -1)
 
     def onward(j, a):
-        take(4 + 4 * j, a, -1, full)
-        send2(6 + 4 * j, a, -1, lo, 1)
-        take(5 + 4 * j, a, 1, full)
-        send2(7 + 4 * j, a, 1, hi, -1)
+        take(3 + 3 * j, a, -1, full)
+        send2(5 + 3 * j, a, -1, lo, 1)
+        take(4 + 3 * j, a, 1, full)
+        send2(5 + 3 * j, a, 1, hi, -1)
 
     def last(j, a):
-        take(6 + 4 * j, a, 2, lo)
-        take(7 + 4 * j, a, 2, hi)
+        take(5 + 3 * j, a, 2, full)
 
     def s0():
         send1(0, 0, 0, full, 1)
@@ -103,7 +102,7 @@
         take(0, -1, 0, full)
         send1(2, -1, 0, lo, 1)
         take(1, 1, 0, full)
-        send1(3, 1, 0, hi, -1)
+        send1(2, 1, 0, hi, -1)
         spread(1, -1)
         spread(2, 1)
 
@@ -111,8 +110,7 @@
         onward(0, 0)
 
     def s4():
-        take(2, 2, 0, lo)
-        take(3, 2, 0, hi)
+        take(2, 2, 0, full)
         spread(3, 2)
 
     def s5():
@@ -199,7 +197,7 @@
 
     sqc = Copies(sq_s, sq_r)
     for i in range(1, 8):
-        sqc.send(i - 1, sq, sqr.at[i - 1], (w, lax.rem(n + i, 8)))
+        sqc.send(0, sq, sqr.at[i - 1], (w, lax.rem(n + i, 8)))
     loads[5].start()
     loads[6].start()
 
@@ -215,8 +213,7 @@
         sine = jnp.sin(angle)
         turns.append((jnp.cos(angle), jnp.where(left, -sine, sine)))
 
-    for i in range(1, 8):
-        sqc.take(i - 1, sqr.at[i - 1], other)
+    sqc.take(0, sqr, other)
     total = sq[...]
     for i in range(7):
         total = total + sqr[i]
@@ -236,8 +233,8 @@
     ag = Copies(ag_s, ag_r)
     ways = [
         [
-            gather_half(ag, r * 40, buf, r, 0, along_x, along_z),
-            gather_half(ag, r * 40 + 20, buf, r, 1, along_z, along_x),
+            gather_half(ag, r * 30, buf, r, 0, along_x, along_z),
+            gather_half(ag, r * 30 + 15, buf, r, 1, along_z, along_x),
         ]
         for r in range(2)
     ]
@@ -265,35 +262,32 @@
         ex.send(2 * r + m, part.at[r, 1 - c, :, at], pair.at[r, :, at], other)
 
     def ring1(r, m):
-        k = 6 * (2 * r + m)
+        k = 3 * (2 * r + m)
         at, lo, hi = pl.ds(4 * m, 4), pl.ds(4 * m, 2), pl.ds(4 * m + 2, 2)
         ex.take(2 * r + m, pair.at[r, :, at], other)
         part[r, c, :, at] = part[r, c, :, at] + pair[r, :, at]
         rs.send(k + 0, part.at[r, c, far, lo], ring_o.at[r, 0, m], up)
         rs.send(k + 1, part.at[r, c, far, hi], ring_o.at[r, 1, m], down)
         rs.send(k + 2, part.at[r, c, above, hi], ring_n.at[r, 0, hi], up)
-        rs.send(k + 3, part.at[r, c, below, lo], ring_n.at[r, 1, lo], down)
+        rs.send(k + 2, part.at[r, c, below, lo], ring_n.at[r, 1, lo], down)
 
     def ring2(r, m):
-        k = 6 * (2 * r + m)
+        k = 3 * (2 * r + m)
         lo, hi = pl.ds(4 * m, 2), pl.ds(4 * m + 2, 2)
         rs.take(k + 0, ring_o.at[r, 0, m], up)
         part[r, c, above, lo] = part[r, c, above, lo] + ring_o[r, 0, m]
-        rs.send(k + 4, part.at[r, c, above, lo], ring_n.at[r, 0, lo], up)
+        rs.send(k + 2, part.at[r, c, above, lo], ring_n.at[r, 0, lo], up)
         rs.take(k + 1, ring_o.at[r, 1, m], up)
         part[r, c, below, hi] = part[r, c, below, hi] + ring_o[r, 1, m]
-        rs.send(k + 5, part.at[r, c, below, hi], ring_n.at[r, 1, hi], down)
+        rs.send(k + 2, part.at[r, c, below, hi], ring_n.at[r, 1, hi], down)
 
     def shift(a, b):
         return jnp.where(y < 2, b, a), jnp.where(y < 2, a, b)
 
     def finish(r, m):
-        k = 6 * (2 * r + m)
-        at, lo, hi = pl.ds(4 * m, 4), pl.ds(4 * m, 2), pl.ds(4 * m + 2, 2)
-        rs.take(k + 2, ring_n.at[r, 0, hi], up)
-        rs.take(k + 3, ring_n.at[r, 1, lo], up)
-        rs.take(k + 4, ring_n.at[r, 0, lo], up)
-        rs.take(k + 5, ring_n.at[r, 1, hi], up)
+        k = 3 * (2 * r + m)
+        at = pl.ds(4 * m, 4)
+        rs.take(k + 2, ring_n.at[r, :, at], up)
         qsend[r, at] = (part[r, c, y, at] + ring_n[r, 0, at] + ring_n[r, 1, at]).astype(BF16)
         for i in (2 * m, 2 * m + 1):
             for s, (a, b) in enumerate(SLOTS[i]):
@@ -303,14 +297,13 @@
                     continue
                 dz, dx = shift(a, b)
                 target = (m4(z + dz) * 4 + m4(x + dx), n)
-                aa.send(16 * r + k, qsend.at[r, k // 2], qrecv.at[r, k], target)
+                aa.send(r, qsend.at[r, k // 2], qrecv.at[r, k], target)
 
     def receive(r):
+        aa.take(r, qrecv.at[r, pl.ds(1, 15)], other)
         for i in range(4):
             for s, (a, b) in enumerate(SLOTS[i]):
                 k = 4 * i + s
-                if k:
-                    aa.take(16 * r + k, qrecv.at[r, k], other)
                 dz, dx = shift(a, b)
                 tile = qrecv[r, k].astype(F32)
                 if s % 2:
@@ -398,37 +391,30 @@
     def spread_heads(r):
         for i in range(1, 16):
             peer = lax.rem(w + i, 16)
-            ao.send(15 * r + i - 1, att.at[r, peer], g.at[r, n, w], (peer, n))
+            ao.send(r, att.at[r, peer], g.at[r, n, w], (peer, n))
         g[r, n, w] = att[r, w]
 
     def narrow1(r):
-        k = 10 * r
-        for i in range(1, 16):
-            ao.take(15 * r + i - 1, g.at[r, n, lax.rem(w - i + 16, 16)], other)
+        k = 3 * r
+        ao.take(r, g.at[r, n, pl.ds(0, 15)], other)
         gn.send(k + 0, g.at[r, n], g.at[r, n], up)
         gn.send(k + 1, g.at[r, n], g.at[r, n], down)
         gn.send(k + 2, g.at[r, n], g.at[r, n], other)
 
     def narrow2(r):
-        k = 10 * r
+        k = 3 * r
         gn.take(k + 0, g.at[r, nb], up)
-        gn.send(k + 3, g.at[r, nb, lo8], g.at[r, nb, lo8], up)
-        gn.send(k + 8, g.at[r, nb, lo8], g.at[r, nb, lo8], up2)
-        gn.send(k + 4, g.at[r, nb], g.at[r, nb], other)
+        gn.send(k + 2, g.at[r, nb, lo8], g.at[r, nb, lo8], up)
+        gn.send(k + 2, g.at[r, nb, lo8], g.at[r, nb, lo8], up2)
+        gn.send(k + 2, g.at[r, nb], g.at[r, nb], other)
         gn.take(k + 1, g.at[r, na], up)
-        gn.send(k + 5, g.at[r, na, hi8], g.at[r, na, hi8], down)
-        gn.send(k + 9, g.at[r, na, hi8], g.at[r, na, hi8], down2)
-        gn.send(k + 6, g.at[r, na], g.at[r, na], other)
+        gn.send(k + 2, g.at[r, na, hi8], g.at[r, na, hi8], down)
+        gn.send(k + 2, g.at[r, na, hi8], g.at[r, na, hi8], down2)
+        gn.send(k + 2, g.at[r, na], g.at[r, na], other)
 
     def narrow3(r):
-        k = 10 * r
-        gn.take(k + 3, g.at[r, nf, lo8], up)
-        gn.take(k + 5, g.at[r, nf, hi8], up)
-        gn.take(k + 2, g.at[r, y * 2 + 1 - c], up)
-        gn.take(k + 4, g.at[r, below * 2 + 1 - c], up)
-        gn.take(k + 6, g.at[r, above * 2 + 1 - c], up)
-        gn.take(k + 8, g.at[r, far * 2 + 1 - c, lo8], up)
-        gn.take(k + 9, g.at[r, far * 2 + 1 - c, hi8], up)
+        k = 3 * r
+        gn.take(k + 2, g.at[r, pl.ds(0, 5)], up)
 
         def regroup(i, carry):
             v = g[r, :, i].astype(F32).reshape(4, 2, 8, 256)
@@ -457,7 +443,7 @@
 
     def products(r):
         for h, index, to1, to2 in halves:
-            k = 24 * r + 12 * h
+            k = 12 * r + 6 * h
             v = product(h, index, 2)
             so[r, h, 0] = v[:, 0:16].astype(BF16)
             so[r, h, 1] = v[:, 16:32].astype(BF16)
@@ -465,7 +451,7 @@
                 st.send(k + u, so.at[r, h, 0, q], ro.at[r, h, 0, q], to1(1))
                 st.send(k + 2 + u, so.at[r, h, 1, q], ro.at[r, h, 1, q], to1(-1))
         for h, index, to1, to2 in halves:
-            k = 24 * r + 12 * h
+            k = 12 * r + 6 * h
             v = product(h, index, 1)
             sn[r, h, 0, :, 16:32] = v[:, 16:32].astype(BF16)
             kp[r, h, 0] = v[:, 0:16]
@@ -478,7 +464,7 @@
             kp[r, h, 1] = v[:, 16:32]
             for u, q in enumerate(two):
                 st.send(
-                    k + 6 + u, sn.at[r, h, 1, q, top16], rn.at[r, h, 1, q, top16], to1(-1)
+                    k + 4 + u, sn.at[r, h, 1, q, top16], rn.at[r, h, 1, q, top16], to1(-1)
                 )
         for h, index, to1, to2 in halves:
             km[r, h] = product(h, index, 0)
@@ -487,26 +473,23 @@
         for u, q in enumerate(two):
             qq = slice(2 * u, 2 * u + 2)
             for h, index, to1, to2 in halves:
-                k = 24 * r + 12 * h
+                k = 12 * r + 6 * h
                 st.take(k + u, ro.at[r, h, 0, q], to1(1))
                 sn[r, h, 0, qq, 0:16] = (
                     kp[r, h, 0, qq] + ro[r, h, 0, qq].astype(F32)
                 ).astype(BF16)
-                st.send(k + 8 + u, sn.at[r, h, 0, q, top16], rn.at[r, h, 0, q, top16], to1(1))
+                st.send(k + 4 + u, sn.at[r, h, 0, q, top16], rn.at[r, h, 0, q, top16], to1(1))
                 st.take(k + 2 + u, ro.at[r, h, 1, q], to1(1))
                 sn[r, h, 1, qq, 16:32] = (
                     kp[r, h, 1, qq] + ro[r, h, 1, qq].astype(F32)
                 ).astype(BF16)
-                st.send(k + 10 + u, sn.at[r, h, 1, q, bot16], rn.at[r, h, 1, q, bot16], to1(-1))
+                st.send(k + 4 + u, sn.at[r, h, 1, q, bot16], rn.at[r, h, 1, q, bot16], to1(-1))
 
     def second(r):
         for u, q in enumerate(two):
             for h, index, to1, to2 in halves:
-                k, k2 = 24 * r + 12 * h, 12 * r + 6 * h
-                st.take(k + 4 + u, rn.at[r, h, 0, q, bot16], to1(1))
-                st.take(k + 6 + u, rn.at[r, h, 1, q, top16], to1(1))
-                st.take(k + 8 + u, rn.at[r, h, 0, q, top16], to1(1))
-                st.take(k + 10 + u, rn.at[r, h, 1, q, bot16], to1(1))
+                k, k2 = 12 * r + 6 * h, 6 * r + 3 * h
+                st.take(k + 4 + u, rn.at[r, h, :, q], to1(1))
                 for i in (2 * u, 2 * u + 1):
                     v = km[r, h, i] + rn[r, h, 0, i].astype(F32) + rn[r, h, 1, i].astype(F32)
                     if i == 0:
@@ -520,25 +503,22 @@
                         st2.send(k2 + 2, sn2.at[r, h, 0, bot16], rn2.at[r, h, 0, bot16], to2(1))
                     elif i == 2:
                         sn2[r, h, 1, 0:16] = v[0:16].astype(BF16)
-                        st2.send(k2 + 3, sn2.at[r, h, 1, top16], rn2.at[r, h, 1, top16], to2(-1))
+                        st2.send(k2 + 2, sn2.at[r, h, 1, top16], rn2.at[r, h, 1, top16], to2(-1))
 
     def relay2(r):
         for h, index, to1, to2 in halves:
-            k2 = 12 * r + 6 * h
+            k2 = 6 * r + 3 * h
             st2.take(k2 + 0, ro2.at[r, h, 0], to1(1))
             sn2[r, h, 0, 0:16] = (km[r, h, 1, 0:16] + ro2[r, h, 0].astype(F32)).astype(BF16)
-            st2.send(k2 + 4, sn2.at[r, h, 0, top16], rn2.at[r, h, 0, top16], to2(1))
+            st2.send(k2 + 2, sn2.at[r, h, 0, top16], rn2.at[r, h, 0, top16], to2(1))
             st2.take(k2 + 1, ro2.at[r, h, 1], to1(1))
             sn2[r, h, 1, 16:32] = (km[r, h, 2, 16:32] + ro2[r, h, 1].astype(F32)).astype(BF16)
-            st2.send(k2 + 5, sn2.at[r, h, 1, bot16], rn2.at[r, h, 1, bot16], to2(-1))
+            st2.send(k2 + 2, sn2.at[r, h, 1, bot16], rn2.at[r, h, 1, bot16], to2(-1))
 
     def total_rows(r):
         for h, index, to1, to2 in halves:
-            k2 = 12 * r + 6 * h
-            st2.take(k2 + 2, rn2.at[r, h, 0, bot16], to1(1))
-            st2.take(k2 + 3, rn2.at[r, h, 1, top16], to1(1))
-            st2.take(k2 + 4, rn2.at[r, h, 0, top16], to1(1))
-            st2.take(k2 + 5, rn2.at[r, h, 1, bot16], to1(1))
+            k2 = 6 * r + 3 * h
+            st2.take(k2 + 2, rn2.at[r, h], to1(1))
             for j in range(8):
                 sub = slice(j * 128, j * 128 + 128)
                 res[h * 8 + j] = (
@@ -597,31 +577,31 @@
     multiply(1, 1)
     ring1(1, 0)
     ring2(0, 1)
+    ring1(1, 1)
     ring2(1, 0)
     finish(0, 1)
-    ring1(1, 1)
     finish(1, 0)
     ring2(1, 1)
     receive(0)
     loads[5].wait()
     loads[6].wait()
+    finish(1, 1)
     attend(0, 0)
-    finish(1, 1)
     attend(0, 1)
     spread_heads(0)
     receive(1)
     attend(1, 0)
-    narrow1(0)
     attend(1, 1)
     spread_heads(1)
+    narrow1(0)
     new_rows()
+    loads[4].wait()
     narrow2(0)
-    loads[4].wait()
+    narrow1(1)
     narrow3(0)
     products(0)
-    narrow1(1)
+    narrow2(1)
     relay(0)
-    narrow2(1)
     narrow3(1)
     second(0)
     products(1)
@@ -672,9 +652,8 @@
             b16(2, 2, 2, 16, 1024), b16(2, 2, 2, 32, 1024),
             b16(2, 2, 2, 16, 1024), b16(2, 2, 2, 32, 1024),
             f32(16, 32, 128), f32(16, 4, 16, 128),
-            dma((11,)), dma((7,)), dma((7,)), dma((80,)), dma((80,)), dma((4,)), dma((4,)),
-            dma((24,)), dma((24,)), dma((32,)), dma((32,)), dma((30,)), dma((30,)),
-            dma((20,)), dma((20,)), dma((48,)), dma((48,)), dma((24,)), dma((24,)),
+            dma((11,)), dma, dma((1,)), dma, dma((60,)), dma, dma((4,)), dma, dma((12,)), dma,
+            dma((2,)), dma, dma((2,)), dma, dma((6,)), dma, dma((24,)), dma, dma((12,)),
         ],
         compiler_params=pltpu.CompilerParams(
             collective_id=0, has_side_effects=True, vmem_limit_bytes=60 << 20

time: 110 us -> 106 us (0.964)
  Pallas kernels: 105 us -> 99.9 us
    pallas_call x1, Pallas kernels: 105 us -> 99.9 us  [local(): pl.pallas_call(layer_kernel, out_shape=(jax.ShapeDtypeStruct((4, 16, 2048...]
where the time goes in v5:
time: 106 us; the launch traced here: 105 us
  Pallas kernels  99.9 us (94%)
  local copies, waits for them, and re-layouts  4.27 us (4%)
    pallas_call x1, Pallas kernels, local(): pl.pallas_call(layer_kernel, out_shape=(jax.ShapeDtypeStruct((4, 16, 2048...  99.9 us
    unnamed x3, local copies, waits for them, and re-layouts  4.27 us

profile of v5, /device:TPU:0, one launch (start us, length us, event | category | flops | bytes accessed | tf_op | source)
XLA Modules:
  0.0 104.8 jit_solution(16788875719709297075)
XLA Ops:
  0.6 99.9 %layer.1 = (bf16[4,16,2048]{2,1,0:T(8,128)(2,1)}, bf16[4,2,512]{2,1,0:T(2,128)(2,1)}, bf16[4,2,512]{2,1,0:T(2,128)(2,1)}) custom-call(s32[2]{0:T(128)} %len_ref.1, s32[2]{0:T(128)} %pos_ref.1, bf16[4,16,2048]{2,1,0:T(8,128)(2,1)} %x_hbm.1, bf16[2048]{0:T(1024)(128)(2,1)} %gain_hbm.1, bf16[2048,512]{1,0:T(8,128)(2,1)} %wq_hbm.1, bf16[64,2048]{1,0:T(8,128)(2,1)} %bitcast.1, ...), custom_call_target="tpu_custom_call" | custom-call | tf_op jit(solution)/shard_map/layer/pallas_call | solution.py:631
  100.5 1.7 %copy.15 = bf16[4,16,2048]{2,1,0:T(8,128)(2,1)} copy(bf16[4,16,2048]{2,1,0:T(8,128)(2,1)} %get-tuple-element.6) | data formatting | bytes 524288
  102.2 1.3 %copy.16 = bf16[4,2,512]{2,1,0:T(2,128)(2,1)} copy(bf16[4,2,512]{2,1,0:T(2,128)(2,1)} %get-tuple-element.7) | data formatting | bytes 16384
  103.5 1.3 %copy.17 = bf16[4,2,512]{2,1,0:T(2,128)(2,1)} copy(bf16[4,2,512]{2,1,0:T(2,128)(2,1)} %get-tuple-element.8) | data formatting | bytes 16384

commit v6 on v5

--- a/solution.py
+++ b/solution.py
@@ -553,47 +553,46 @@
 
     stores = []
 
-    gather(0, 0, 1, 2)
+    gather(0, 0, 1, 2, 3)
     gather(1, 0, 1)
-    gather(0, 3, 4)
-    gather(1, 2)
-    gather(0, 5)
+    gather(0, 4, 5)
     loads[2].wait()
     loads[3].wait()
     multiply(0, 0)
-    gather(1, 3)
     gather(0, 6)
-    gather(1, 4)
+    gather(1, 2)
     ring1(0, 0)
     gather(0, 7)
     multiply(0, 1)
+    gather(1, 3)
+    ring2(0, 0)
+    gather(1, 4)
+    ring1(0, 1)
     gather(1, 5)
-    ring2(0, 0)
     multiply(1, 0)
+    finish(0, 0)
     gather(1, 6)
-    finish(0, 0)
-    ring1(0, 1)
+    ring2(0, 1)
     gather(1, 7)
     multiply(1, 1)
     ring1(1, 0)
-    ring2(0, 1)
+    finish(0, 1)
     ring1(1, 1)
     ring2(1, 0)
-    finish(0, 1)
-    finish(1, 0)
     ring2(1, 1)
     receive(0)
     loads[5].wait()
     loads[6].wait()
+    attend(0, 0)
+    finish(1, 0)
     finish(1, 1)
-    attend(0, 0)
     attend(0, 1)
     spread_heads(0)
     receive(1)
     attend(1, 0)
+    narrow1(0)
     attend(1, 1)
     spread_heads(1)
-    narrow1(0)
     new_rows()
     loads[4].wait()
     narrow2(0)
@@ -603,8 +602,8 @@
     narrow2(1)
     relay(0)
     narrow3(1)
+    products(1)
     second(0)
-    products(1)
     relay(1)
     relay2(0)
     second(1)

time: 106 us -> 99.9 us (0.942)
  Pallas kernels: 99.9 us -> 94.8 us
    pallas_call x1, Pallas kernels: 99.9 us -> 94.8 us  [local(): pl.pallas_call(layer_kernel, out_shape=(jax.ShapeDtypeStruct((4, 16, 2048...]
where the time goes in v6:
time: 99.9 us; the launch traced here: 99.7 us
  Pallas kernels  94.8 us (95%)
  local copies, waits for them, and re-layouts  4.27 us (4%)
    pallas_call x1, Pallas kernels, local(): pl.pallas_call(layer_kernel, out_shape=(jax.ShapeDtypeStruct((4, 16, 2048...  94.8 us
    unnamed x3, local copies, waits for them, and re-layouts  4.27 us

profile of v6, /device:TPU:0, one launch (start us, length us, event | category | flops | bytes accessed | tf_op | source)
XLA Modules:
  0.0 99.7 jit_solution(14011370538136168828)
XLA Ops:
  0.6 94.8 %layer.1 = (bf16[4,16,2048]{2,1,0:T(8,128)(2,1)}, bf16[4,2,512]{2,1,0:T(2,128)(2,1)}, bf16[4,2,512]{2,1,0:T(2,128)(2,1)}) custom-call(s32[2]{0:T(128)} %len_ref.1, s32[2]{0:T(128)} %pos_ref.1, bf16[4,16,2048]{2,1,0:T(8,128)(2,1)} %x_hbm.1, bf16[2048]{0:T(1024)(128)(2,1)} %gain_hbm.1, bf16[2048,512]{1,0:T(8,128)(2,1)} %wq_hbm.1, bf16[64,2048]{1,0:T(8,128)(2,1)} %bitcast.1, ...), custom_call_target="tpu_custom_call" | custom-call | tf_op jit(solution)/shard_map/layer/pallas_call | solution.py:630
  95.4 1.7 %copy.15 = bf16[4,16,2048]{2,1,0:T(8,128)(2,1)} copy(bf16[4,16,2048]{2,1,0:T(8,128)(2,1)} %get-tuple-element.6) | data formatting | bytes 524288
  97.1 1.3 %copy.16 = bf16[4,2,512]{2,1,0:T(2,128)(2,1)} copy(bf16[4,2,512]{2,1,0:T(2,128)(2,1)} %get-tuple-element.7) | data formatting | bytes 16384
  98.4 1.3 %copy.17 = bf16[4,2,512]{2,1,0:T(2,128)(2,1)} copy(bf16[4,2,512]{2,1,0:T(2,128)(2,1)} %get-tuple-element.8) | data formatting | bytes 16384

commit v7 on v6

--- a/solution.py
+++ b/solution.py
@@ -140,8 +140,8 @@
 
 def layer_kernel(
     len_ref, pos_ref, x_hbm, gain_hbm, wq_hbm, wkv_hbm, wo_hbm, k_hbm, v_hbm,
-    out_hbm, nk_hbm, nv_hbm,
-    out_ref, nk, nv, xv, gain, wq, wkv, wo, kb, vb,
+    out_hbm, new_hbm,
+    out_ref, new, xv, gain, wq, wkv, wo, kb, vb,
     xs, sq, sqr, buf, part, pair, ring_o, ring_n, qsend, qrecv, qx,
     qs, kf, vf, kvout, sc, att, g, gm,
     so, sn, ro, rn, kp, km, so2, sn2, ro2, rn2, res, rows16,
@@ -535,7 +535,7 @@
                         out_ref[t, :, j * 128 : j * 128 + 128] = rows16[j, t].astype(BF16)
                 cols = pl.ds(h * 1024, 1024)
                 store = pltpu.make_async_copy(
-                    out_ref.at[:, :, cols], out_hbm.at[:, :, cols], ld.at[9 + h]
+                    out_ref.at[:, :, cols], out_hbm.at[:, :, cols], ld.at[8 + h]
                 )
                 store.start()
                 stores.append(store)
@@ -544,12 +544,11 @@
         for t in range(4):
             for h in range(4):
                 cols = slice(h * 128, h * 128 + 128)
-                nk[t, :, cols] = kvout[0, h, 2 * t : 2 * t + 2].astype(BF16)
-                nv[t, :, cols] = kvout[1, h, 2 * t : 2 * t + 2].astype(BF16)
-        for i, (source, target) in enumerate(((nk, nk_hbm), (nv, nv_hbm))):
-            store = pltpu.make_async_copy(source, target, ld.at[7 + i])
-            store.start()
-            stores.append(store)
+                for i in range(2):
+                    new[i, t, :, cols] = kvout[i, h, 2 * t : 2 * t + 2].astype(BF16)
+        store = pltpu.make_async_copy(new, new_hbm, ld.at[7])
+        store.start()
+        stores.append(store)
 
     stores = []
 
@@ -627,17 +626,16 @@
     def f32(*shape):
         return pltpu.VMEM(shape, F32)
 
-    return pl.pallas_call(
+    attended, new = pl.pallas_call(
         layer_kernel,
         out_shape=(
             jax.ShapeDtypeStruct((4, 16, 2048), BF16),
-            jax.ShapeDtypeStruct((4, 2, 512), BF16),
-            jax.ShapeDtypeStruct((4, 2, 512), BF16),
+            jax.ShapeDtypeStruct((2, 4, 2, 512), BF16),
         ),
         in_specs=[sm, sm] + [hbm] * 7,
-        out_specs=(hbm, hbm, hbm),
+        out_specs=(hbm, hbm),
         scratch_shapes=[
-            b16(4, 16, 2048), b16(4, 2, 512), b16(4, 2, 512),
+            b16(4, 16, 2048), b16(2, 4, 2, 512),
             b16(4, 16, 2048), b16(2048), b16(2048, 512), b16(64, 2048), b16(512, 2048),
             b16(2, 4096, 512), b16(2, 4096, 512),
             f32(16, 64, 128), f32(8, 128), f32(7, 8, 128), b16(2, 4, 2, 4, 16, 2048),
@@ -651,7 +649,7 @@
             b16(2, 2, 2, 16, 1024), b16(2, 2, 2, 32, 1024),
             b16(2, 2, 2, 16, 1024), b16(2, 2, 2, 32, 1024),
             f32(16, 32, 128), f32(16, 4, 16, 128),
-            dma((11,)), dma, dma((1,)), dma, dma((60,)), dma, dma((4,)), dma, dma((12,)), dma,
+            dma((10,)), dma, dma((1,)), dma, dma((60,)), dma, dma((4,)), dma, dma((12,)), dma,
             dma((2,)), dma, dma((2,)), dma, dma((6,)), dma, dma((24,)), dma, dma((12,)),
         ],
         compiler_params=pltpu.CompilerParams(
@@ -662,6 +660,7 @@
         lengths, positions, inputs, norm_gain, w_query, w_keyval.T, w_out,
         key_cache, value_cache,
     )
+    return attended, new[0], new[1]
 
 
 def solution(mesh):

time: 99.9 us -> 98.6 us (0.987)
  local copies, waits for them, and re-layouts: 4.27 us -> 3 us
    unnamed x3 -> x1, local copies, waits for them, and re-layouts: 4.27 us -> 1.67 us
    squeeze x0 -> x1, local copies, waits for them, and re-layouts: none -> 1.33 us  [local(): return (attended, new[0], new[1])]
where the time goes in v7:
time: 98.6 us; the launch traced here: 98.4 us
  Pallas kernels  94.7 us (96%)
  local copies, waits for them, and re-layouts  3 us (3%)
    pallas_call x1, Pallas kernels, local(): pl.pallas_call(layer_kernel, out_shape=(jax.ShapeDtypeStruct((4, 16, 2048...  94.7 us

profile of v7, /device:TPU:0, one launch (start us, length us, event | category | flops | bytes accessed | tf_op | source)
XLA Modules:
  0.0 98.4 jit_solution(18069794767323192036)
XLA Ops:
  0.6 94.7 %layer.1 = (bf16[4,16,2048]{2,1,0:T(8,128)(2,1)}, bf16[2,4,2,512]{3,2,1,0:T(2,128)(2,1)}) custom-call(s32[2]{0:T(128)} %len_ref.1, s32[2]{0:T(128)} %pos_ref.1, bf16[4,16,2048]{2,1,0:T(8,128)(2,1)} %x_hbm.1, bf16[2048]{0:T(1024)(128)(2,1)} %gain_hbm.1, bf16[2048,512]{1,0:T(8,128)(2,1)} %wq_hbm.1, bf16[64,2048]{1,0:T(8,128)(2,1)} %bitcast.5, ...), custom_call_target="tpu_custom_call" | custom-call | tf_op jit(solution)/shard_map/layer/pallas_call | solution.py:629
  95.4 1.3 %slice_bitcast_fusion = (bf16[4,2,512]{2,1,0:T(2,128)(2,1)}, bf16[4,2,512]{2,1,0:T(2,128)(2,1)}) fusion(bf16[2,4,2,512]{3,2,1,0:T(2,128)(2,1)} %get-tuple-element.6), kind=kLoop, calls=%fused_computation | loop fusion | bytes 32768 | tf_op jit(solution)/shard_map/squeeze | solution.py:663
  96.7 1.7 %copy.13 = bf16[4,16,2048]{2,1,0:T(8,128)(2,1)} copy(bf16[4,16,2048]{2,1,0:T(8,128)(2,1)} %get-tuple-element.12) | data formatting | bytes 524288
